TPU v7x, 512 devices: a whole 4x4x16 slice. The times are simulated.
512 devices in a mesh: row: 64 (over z_lo, y, x), col: 8 (over z_hi, core).
Axes of the slice: x: 4, y: 4, z: 16 (z_hi: 4, z_lo: 4; z = z_hi * 4 + z_lo), core: 2. Of those that a mesh axis runs over, the one named last changes fastest.
Arguments:
- front: float32 [65536, 1024], P('row', 'col'), may hold values from -6 to 6
- contrib: bfloat16 [524288, 1024], P('row', 'col'), may hold values from -6 to 6
- target: int32 [2048], replicated, may hold values from 0 to 255, as said below
- mask: int32 [256, 8], P('row', 'col'), may hold values 0 or 1
- panel: float32 [65536, 256], P(('row', 'col')), as said below
- pivots: int32 [256], replicated, may hold values from 0 to 65535, as said below
Outputs:
- lower: float32 [65536, 256], P(('row', 'col'))
- schur: float32 [65536, 1024], P('row', 'col')
Inputs may be any that keep to these rules, and one draw needn't show every extreme that they name: Front block row t lies on index t // 4 of row. Within each aligned block of 32 entries (one device's contribution blocks) the values target // 4 are distinct, and index 0 of row receives a block from every aligned block. `pivots`: distinct rows; each aligned group of 1024 rows holds exactly 4 of them. The 256 x 256 matrix formed by the panel's rows named in pivots is invertible.
All inputs are finite; a program needn't handle non-finite values. No bound on the sum of `mask` on one device may be relied on, other than what follows from the above.
Results may differ from a plain program's by a relative error of at most 0.0003.
Values may be sent and summed in bfloat16 or wider, within the bound.
No kernel may reach another device: no remote copies, remote signals or barrier semaphores. Data moves between devices by JAX's collectives and lax.ppermute only.
A program may use at most 64 MiB of HBM per device.

v0:
```python
import jax
import jax.numpy as jnp
from jax import lax
from jax.sharding import PartitionSpec as P

BLK = 256


def exact_dot(left, right):
    return jnp.dot(left, right, precision=lax.Precision.HIGHEST, preferred_element_type=jnp.float32)


def body(front, contrib, target, mask, panel, pivots):
    row_count = lax.axis_size("row")
    col_count = lax.axis_size("col")
    row_index = lax.axis_index("row")
    col_index = lax.axis_index("col")
    tile_rows, tile_cols = front.shape
    blocks_own = tile_rows // BLK
    sent_count = contrib.shape[0] // BLK
    targets = target.reshape(row_count, sent_count)
    own_targets = lax.dynamic_slice_in_dim(targets, row_index, 1, 0)[0]
    device_ids = jnp.arange(row_count, dtype=jnp.int32)
    chooser = (own_targets[None, :] // blocks_own == device_ids[:, None]).astype(jnp.bfloat16)
    pieces = contrib.reshape(sent_count, BLK, tile_cols)
    outgoing = jnp.einsum(
        "db,bxc->dxc", chooser, pieces, preferred_element_type=jnp.float32
    ).astype(jnp.bfloat16)
    arrived = lax.all_to_all(outgoing, "row", split_axis=0, concat_axis=0, tiled=True)
    source_targets = jnp.take(targets, device_ids, axis=0)
    block_ids = jnp.arange(blocks_own, dtype=jnp.int32)
    own_blocks = row_index * blocks_own + block_ids
    placing = jnp.sum(
        (source_targets[:, :, None] == own_blocks[None, None, :]).astype(jnp.float32), axis=1
    ).astype(jnp.bfloat16)
    added = jnp.einsum("sk,sxc->kxc", placing, arrived, preferred_element_type=jnp.float32).reshape(
        tile_rows, tile_cols
    )
    assembled = front + added
    panel_rows = panel.shape[0]
    panel_start = (row_index * col_count + col_index) * panel_rows
    select_rows = (
        pivots[:, None] - panel_start == jnp.arange(panel_rows, dtype=jnp.int32)[None, :]
    ).astype(jnp.float32)
    pivot_block = lax.psum(exact_dot(select_rows, panel), ("row", "col"))
    gram = exact_dot(pivot_block, pivot_block.T)
    factor_low = jnp.linalg.cholesky(gram)
    inverse = jax.scipy.linalg.cho_solve((factor_low, True), pivot_block).T
    local_start = row_index * tile_rows
    picker = (
        pivots[:, None] - local_start == jnp.arange(tile_rows, dtype=jnp.int32)[None, :]
    ).astype(jnp.float32)
    upper = lax.psum(exact_dot(picker, assembled), "row")
    lower_own = exact_dot(panel, inverse)
    update = exact_dot(lax.all_gather(lower_own, "col", axis=0, tiled=True), upper)
    row_mask = jnp.repeat(mask[:, 0].astype(jnp.float32), BLK)
    schur = assembled - row_mask[:, None] * update
    return (lower_own, schur)


def solution(mesh):
    placed = (P("row", "col"), P("row", "col"), P(), P("row", "col"), P(("row", "col"), None), P())
    return jax.shard_map(
        body,
        mesh=mesh,
        in_specs=placed,
        out_specs=(P(("row", "col"), None), P("row", "col")),
        check_vma=False,
    )
```

profile of v0, /device:TPU:2, one launch (start us, length us, event | category | flops | bytes accessed | tf_op | source)
XLA Modules:
  0.0 1228.4 jit_solution(2532103232973570547)
XLA Ops:
  8.0 0.9 reshape.68
  8.9 0.7 copy-done
  9.6 1.8 convolution_convert_fusion
  11.4 4.7 copy.22
  16.1 12.4 %all-to-all-start = ((bf16[64,256,128]{2,1,0:T(8,128)(2,1)}), bf16[64,256,128]{2,1,0:T(8,128)(2,1)}, u32[]{:S(2)}, u32[]{:S(2)}) async-start(bf16[64,256,128]{2,1,0:T(8,128)(2,1)} %copy.22), calls=%async_computation | async-start | bytes 8388608 | tf_op jit(solution)/shard_map/all_to_all | solution.py:29
  28.6 1.0 fusion.12
  29.9 474.1 %all-reduce.4.cloned.1.call-done = f32[256,256]{1,0:T(8,128)} async-done(((f32[256,256]{1,0:T(8,128)}), f32[256,256]{1,0:T(8,128)}) %all-reduce.4.cloned.1.call-update) | async-done | bytes 262160 | tf_op jit(solution)/shard_map/psum | solution.py:45
  504.0 1.5 fusion.30
  505.7 11.7 cholesky.50
  517.5 9.8 custom-call.18
  527.7 11.7 cholesky.105
  539.5 0.7 compare_reduce_fusion
  541.6 4.2 while.1
  542.4 1.4 bitcast_dynamic-update-slice_fusion.2
  544.5 1.4 bitcast_dynamic-update-slice_fusion.2
  545.9 0.6 copy-done.6
  546.5 20.5 %custom-call.19 = f32[2,128,128]{1,2,0:T(8,128)S(1)} custom-call(f32[2,128,128]{2,1,0:T(8,128)} %copy-done.6), custom_call_target="InvertDiagBlocksLowerTriangular" | custom-call | tf_op jit(solution)/shard_map/jit(_cho_solve)/triangular_solve | solution.py:48
  568.8 1.0 convolution_bitcast_fusion
  570.8 4.5 fusion
  575.5 1.3 fusion.4
  576.9 0.8 copy.25
  577.7 41.3 %all-gather.2.cloned.1.call-done = f32[1024,256]{0,1:T(8,128)} async-done(((f32[128,256]{0,1:T(8,128)}), f32[1024,256]{0,1:T(8,128)}) %all-gather.2.cloned.1.call-update) | async-done | bytes 1048592 | tf_op jit(solution)/shard_map/all_gather | solution.py:55
  619.0 598.1 %all-reduce.6.cloned.1.call-done = f32[256,128]{1,0:T(8,128)} async-done(((f32[256,128]{1,0:T(8,128)}), f32[256,128]{1,0:T(8,128)}) %all-reduce.6.cloned.1.call-update) | async-done | bytes 131088 | tf_op jit(solution)/shard_map/psum | solution.py:53
  1217.1 3.9 fusion.3
  (58 shorter events, 5.2 us)
Async XLA Ops:
  8.0 1.6 copy-start
  16.1 12.5 %copy-start.5 = (s32[256]{0:T(256)S(1)}, s32[256]{0:T(256)}, u32[]{:S(2)}) copy-start(s32[256]{0:T(256)} %param.11) | copy-start | bytes 3076
  16.1 12.5 %copy-start.4 = (f32[128,256]{1,0:T(8,128)S(1)}, f32[128,256]{1,0:T(8,128)}, u32[]{:S(2)}) copy-start(f32[128,256]{1,0:T(8,128)} %param.10) | copy-start | bytes 393220
  16.1 554.7 %all-to-all-start = ((bf16[64,256,128]{2,1,0:T(8,128)(2,1)}), bf16[64,256,128]{2,1,0:T(8,128)(2,1)}, u32[]{:S(2)}, u32[]{:S(2)}) async-start(bf16[64,256,128]{2,1,0:T(8,128)(2,1)} %copy.22), calls=%async_computation | async-start | bytes 8388608 | tf_op jit(solution)/shard_map/all_to_all | solution.py:29
  28.5 475.4 %all-reduce.4.cloned.1.call-start = ((), (), s32[]{:S(2)}) async-start(), calls=%async_computation.1 | async-start | bytes 524288 | tf_op jit(solution)/shard_map/psum | solution.py:45
  29.6 541.2 %copy-start.7 = (s32[4,1]{0,1:T(1,128)S(1)}, s32[4,1]{0,1:T(1,128)}, u32[]{:S(2)}) copy-start(s32[4,1]{0,1:T(1,128)} %param.9) | copy-start | bytes 52
  29.7 589.3 %all-gather.2.cloned.1.call-start = ((), (), s32[]{:S(2)}) async-start(), calls=%async_computation.2 | async-start | bytes 1179648 | tf_op jit(solution)/shard_map/all_gather | solution.py:55
  504.0 63.1 %copy-start.1 = (f32[256,256]{1,0:T(8,128)S(1)}, f32[256,256]{1,0:T(8,128)}, u32[]{:S(2)}) copy-start(f32[256,256]{1,0:T(8,128)} %all-reduce.4.cloned.1.call-done) | copy-start | bytes 786436
  545.9 0.7 copy-start.6
  567.6 7.8 copy-start.3
  569.9 647.2 %all-reduce.6.cloned.1.call-start = ((), (), s32[]{:S(2)}) async-start(), calls=%async_computation.3 | async-start | bytes 262144 | tf_op jit(solution)/shard_map/psum | solution.py:53
  570.5 6.4 copy-start.2
Sparse Core Ops, SparseCore 0:
  35.4 468.5 all-reduce.3
  570.0 48.9 all-gather.1
Sparse Core Ops, SparseCore 1:
  576.9 640.1 all-reduce.5
where the time goes:
time: 1230 us
  waiting for transfers between devices  1110 us (90%)
  other arithmetic  54.8 us (4%)
  matrix products  17.3 us (1%)
  between operations  17.1 us (1%)
  local copies, waits for them, and re-layouts  12.7 us (1%)
  starting transfers between devices  12.7 us (1%)
    psum x1, waiting for transfers between devices, body(): upper = lax.psum(exact_dot(picker, assembled), 'row')  598 us
    psum x1, waiting for transfers between devices, body(): pivot_block = lax.psum(exact_dot(select_rows, panel), ('row', 'col'))  474 us
    all_gather x1, waiting for transfers between devices, body(): lax.all_gather(lower_own, 'col', axis=0, tiled=True)  41.3 us
    another operation x6, other arithmetic, body(): factor_low = jnp.linalg.cholesky(gram)  34 us
  transfers between devices with their start and end apart: 4, of which 3 were waited for; matrix products, arithmetic and copies ran while one was open for 6% of the time, Pallas kernels for 0%

commit v1 on v0

v1 whole, which is shorter than its diff:
```python
import jax
import jax.numpy as jnp
from jax import lax
from jax.sharding import PartitionSpec as P

BLK = 256


def exact_dot(left, right):
    return jnp.dot(left, right, precision=lax.Precision.HIGHEST, preferred_element_type=jnp.float32)


def spread_rows(rows):
    count = lax.axis_size("row")
    sent = jnp.broadcast_to(rows[None], (count,) + rows.shape)
    return lax.all_to_all(sent, "row", split_axis=0, concat_axis=0, tiled=True).reshape(-1, rows.shape[-1])


def sum_over_col(value):
    count = lax.axis_size("col")
    step = 1
    while step < count:
        value = value + lax.ppermute(value, "col", [(c, c ^ step) for c in range(count)])
        step *= 2
    return value


def body(front, contrib, target, mask, panel, pivots):
    row_count = lax.axis_size("row")
    row_index = lax.axis_index("row")
    col_index = lax.axis_index("col")
    tile_rows, tile_cols = front.shape
    blocks_own = tile_rows // BLK
    sent_count = contrib.shape[0] // BLK
    targets = target.reshape(row_count, sent_count)

    width = pivots.shape[0]
    own_count = width // row_count
    rank = jnp.sum((pivots[:, None] > pivots[None, :]).astype(jnp.int32), axis=1)
    order = rank[None, :] == jnp.arange(width, dtype=jnp.int32)[:, None]
    own_slots = row_index * own_count + jnp.arange(own_count, dtype=jnp.int32)
    own_order = rank[None, :] == own_slots[:, None]
    own_pivots = jnp.sum(jnp.where(own_order, pivots[None, :], 0), axis=1) - row_index * tile_rows

    panel_rows = panel.shape[0]
    select_rows = (
        own_pivots[:, None] - col_index * panel_rows == jnp.arange(panel_rows, dtype=jnp.int32)[None, :]
    ).astype(jnp.float32)
    pivot_sorted = sum_over_col(spread_rows(exact_dot(select_rows, panel)))

    own_targets = lax.dynamic_slice_in_dim(targets, row_index, 1, 0)[0]
    device_ids = jnp.arange(row_count, dtype=jnp.int32)
    chooser = (own_targets[None, :] // blocks_own == device_ids[:, None]).astype(jnp.bfloat16)
    pieces = contrib.reshape(sent_count, BLK, tile_cols)
    outgoing = jnp.einsum(
        "db,bxc->dxc", chooser, pieces, preferred_element_type=jnp.float32
    ).astype(jnp.bfloat16)
    arrived = lax.all_to_all(outgoing, "row", split_axis=0, concat_axis=0, tiled=True)
    panel_full = lax.all_gather(panel, "col", axis=0, tiled=True)

    gram = exact_dot(pivot_sorted, pivot_sorted.T)
    factor_low = jnp.linalg.cholesky(gram)
    inverse_sorted = jax.scipy.linalg.cho_solve((factor_low, True), pivot_sorted).T
    lower_own = exact_dot(panel, exact_dot(inverse_sorted, order.astype(jnp.float32)))

    block_ids = jnp.arange(blocks_own, dtype=jnp.int32)
    own_blocks = row_index * blocks_own + block_ids
    placing = jnp.sum(
        (targets[:, :, None] == own_blocks[None, None, :]).astype(jnp.float32), axis=1
    ).astype(jnp.bfloat16)
    added = jnp.einsum("sk,sxc->kxc", placing, arrived, preferred_element_type=jnp.float32).reshape(
        tile_rows, tile_cols
    )
    assembled = front + added
    picker = (own_pivots[:, None] == jnp.arange(tile_rows, dtype=jnp.int32)[None, :]).astype(jnp.float32)
    upper_sorted = spread_rows(exact_dot(picker, assembled))
    update = exact_dot(panel_full, exact_dot(inverse_sorted, upper_sorted))
    row_mask = jnp.repeat(mask[:, 0].astype(jnp.float32), BLK)
    schur = assembled - row_mask[:, None] * update
    return (lower_own, schur)


def solution(mesh):
    placed = (P("row", "col"), P("row", "col"), P(), P("row", "col"), P(("row", "col"), None), P())
    return jax.shard_map(
        body,
        mesh=mesh,
        in_specs=placed,
        out_specs=(P(("row", "col"), None), P("row", "col")),
        check_vma=False,
    )
```

time: 1230 us -> 308 us (0.25)
  the two profiles are of different devices: /device:TPU:2 before, /device:TPU:1 now
where the time goes in v1:
time: 308 us; the launch traced here: 307 us
  starting transfers between devices  109 us (35%)
  waiting for transfers between devices  89.2 us (29%)
  other arithmetic  57.8 us (19%)
  matrix products  17.7 us (6%)
  local copies, waits for them, and re-layouts  17.3 us (6%)
  between operations  15.6 us (5%)
    ppermute x3, waiting for transfers between devices, sum_over_col(): lax.ppermute(value, 'col', [(c, c ^ step) for c in range(count)])  78.5 us
    all_to_all x2, starting transfers between devices, spread_rows(): lax.all_to_all(sent, 'row', split_axis=0, concat_axis=0, tiled=True)  77.5 us
    another operation x6, other arithmetic, body(): factor_low = jnp.linalg.cholesky(gram)  34 us
    ppermute x3, starting transfers between devices, sum_over_col(): lax.ppermute(value, 'col', [(c, c ^ step) for c in range(count)])  25.2 us
    another operation x3, other arithmetic, body(): jax.scipy.linalg.cho_solve((factor_low, True), pivot_sorted)  20.5 us
    all_to_all x2, waiting for transfers between devices, spread_rows(): lax.all_to_all(sent, 'row', split_axis=0, concat_axis=0, tiled=True)  10.6 us
    all_to_all x1, starting transfers between devices, body(): lax.all_to_all(outgoing, 'row', split_axis=0, concat_axis=0, tiled=True)  6.71 us
  transfers between devices with their start and end apart: 7, of which 5 were waited for; matrix products, arithmetic and copies ran while one was open for 28% of the time, Pallas kernels for 0%

profile of v1, /device:TPU:1, one launch (start us, length us, event | category | flops | bytes accessed | tf_op | source)
XLA Modules:
  0.0 307.1 jit_solution(9168844855809732874)
XLA Ops:
  10.9 12.6 %all-to-all-start = ((f32[64,4,256]{2,1,0:T(4,128)}), f32[64,4,256]{2,1,0:T(4,128)S(1)}, u32[]{:S(2)}, u32[]{:S(2)}) async-start(f32[64,4,256]{2,1,0:T(4,128)} %broadcast_in_dim.21), calls=%async_computation | async-start | bytes 524288 | tf_op jit(solution)/shard_map/all_to_all | solution.py:16
  24.3 1.8 convolution_convert_fusion
  26.1 4.7 %copy.30 = bf16[64,256,128]{2,1,0:T(8,128)(2,1)} copy(bf16[64,256,128]{2,0,1:T(8,128)(2,1)S(1)} %convolution_convert_fusion) | data formatting | bytes 8388608 | tf_op jit(solution)/shard_map/convert_element_type | solution.py:57
  30.8 3.9 %all-to-all-done = f32[64,4,256]{2,1,0:T(4,128)S(1)} async-done(((f32[64,4,256]{2,1,0:T(4,128)}), f32[64,4,256]{2,1,0:T(4,128)S(1)}, u32[]{:S(2)}, u32[]{:S(2)}) %all-to-all-start) | async-done | bytes 262176 | tf_op jit(solution)/shard_map/all_to_all | solution.py:16
  34.7 6.7 %all-to-all-start.1 = ((bf16[64,256,128]{2,1,0:T(8,128)(2,1)}), bf16[64,256,128]{2,1,0:T(8,128)(2,1)}, u32[]{:S(2)}, u32[]{:S(2)}) async-start(bf16[64,256,128]{2,1,0:T(8,128)(2,1)} %copy.30), calls=%async_computation.1 | async-start | bytes 8388608 | tf_op jit(solution)/shard_map/all_to_all | solution.py:58
  41.5 3.4 %collective-permute-start = (f32[256,256]{1,0:T(8,128)S(1)}, f32[256,256]{1,0:T(8,128)S(1)}, u32[]{:S(2)}, u32[]{:S(2)}) collective-permute-start(f32[256,256]{1,0:T(8,128)S(1)} %reshape.65), channel_id=1, source_target_pairs={{0,1},{1,0},{2,3},{3,2},{4,5},{5,4},{6,7},{7,6},{8,9},{9,8},{10,11... | collective-permute-start | bytes 786440 | tf_op jit(solution)/shard_map/ppermute | solution.py:23
  45.0 1.1 collective-permute-done
  46.1 8.8 %collective-permute-start.1 = (f32[256,256]{1,0:T(8,128)S(1)}, f32[256,256]{1,0:T(8,128)S(1)}, u32[]{:S(2)}, u32[]{:S(2)}) collective-permute-start(f32[256,256]{1,0:T(8,128)S(1)} %add.60), channel_id=1, source_target_pairs={{0,2},{1,3},{2,0},{3,1},{4,6},{5,7},{6,4},{7,5},{8,10},{9,11},{10,... | collective-permute-start | bytes 786440 | tf_op jit(solution)/shard_map/ppermute | solution.py:23
  55.0 74.6 %collective-permute-done.1 = f32[256,256]{1,0:T(8,128)S(1)} collective-permute-done((f32[256,256]{1,0:T(8,128)S(1)}, f32[256,256]{1,0:T(8,128)S(1)}, u32[]{:S(2)}, u32[]{:S(2)}) %collective-permute-start.1) | collective-permute-done | bytes 262176 | tf_op jit(solution)/shard_map/ppermute | solution.py:23
  129.6 12.9 %collective-permute-start.2 = (f32[256,256]{1,0:T(8,128)S(1)}, f32[256,256]{1,0:T(8,128)S(1)}, u32[]{:S(2)}, u32[]{:S(2)}) collective-permute-start(f32[256,256]{1,0:T(8,128)S(1)} %add.61), channel_id=1, source_target_pairs={{0,4},{1,5},{2,6},{3,7},{4,0},{5,1},{6,2},{7,3},{8,12},{9,13},{10,... | collective-permute-start | bytes 786440 | tf_op jit(solution)/shard_map/ppermute | solution.py:23
  142.7 1.2 copy.33
  144.0 2.8 collective-permute-done.2
  148.2 11.7 %cholesky.50 = f32[128,128]{1,0:T(8,128)S(1)} custom-call(f32[128,128]{1,0:T(8,128)S(1)} %cholesky.118), custom_call_target="Cholesky" | custom-call | tf_op jit(solution)/shard_map/jit(cholesky)/cholesky | solution.py:62
  160.0 9.8 %custom-call.18 = f32[1,128,128]{1,2,0:T(8,128)S(1)} custom-call(f32[1,128,128]{2,1,0:T(8,128)S(1)} %get-tuple-element.33), custom_call_target="InvertDiagBlocksLowerTriangular" | custom-call | tf_op jit(solution)/shard_map/jit(cholesky)/cholesky | solution.py:62
  172.0 11.7 %cholesky.105 = f32[128,128]{1,0:T(8,128)S(1)} custom-call(f32[128,128]{1,0:T(8,128)S(1)} %slice_subtract_fusion.2), custom_call_target="Cholesky" | custom-call | tf_op jit(solution)/shard_map/jit(cholesky)/cholesky | solution.py:62
  185.8 5.3 %while.1 = (s32[]{:T(128)}, f32[256,256]{1,0:T(8,128)S(1)}, s32[2,2]{1,0:T(2,128)S(1)}, f32[2,128,128]{2,1,0:T(8,128)}, s32[]{:T(128)}) while((s32[]{:T(128)}, f32[256,256]{1,0:T(8,128)S(1)}, s32[2,2]{1,0:T(2,128)S(1)}, f32[2,128,128]{2,1,0:T(8,128)}, s32[]{:T(128)}) %tuple.32), condition=%wide.while_cond, body=%wide.while_body.sunk | while | flops 2 | bytes 132705 | solution.py:63
  186.6 2.0 bitcast_dynamic-update-slice_fusion.2
  189.2 2.0 bitcast_dynamic-update-slice_fusion.2
  191.2 20.5 %custom-call.19 = f32[2,128,128]{1,2,0:T(8,128)S(1)} custom-call(f32[2,128,128]{2,1,0:T(8,128)} %get-tuple-element.9), custom_call_target="InvertDiagBlocksLowerTriangular" | custom-call | tf_op jit(solution)/shard_map/jit(_cho_solve)/triangular_solve | solution.py:63
  213.8 4.6 %fusion = f32[4,256,128]{2,0,1:T(4,128)S(1)} fusion(bf16[64,256,128]{2,1,0:T(8,128)(2,1)} %all-to-all-done.1, bf16[64,4]{0,1:T(4,128)(2,1)S(1)} %convert_reduce_fusion.1), kind=kOutput, calls=%fused_computation.2 | convolution fusion | flops 16777216 | bytes 4719104 | tf_op jit(solution)/shard_map/sk,sxc->kxc/dot_general | solution.py:71
  221.5 64.9 %all-to-all-start.2 = ((f32[64,4,128]{2,1,0:T(4,128)}), f32[64,4,128]{2,1,0:T(4,128)S(1)}, u32[]{:S(2)}, u32[]{:S(2)}) async-start(f32[64,4,128]{2,1,0:T(4,128)} %broadcast_in_dim.24), calls=%async_computation.2 | async-start | bytes 262144 | tf_op jit(solution)/shard_map/all_to_all | solution.py:16
  286.5 1.2 fusion.15
  289.4 6.7 %all-to-all-done.2 = f32[64,4,128]{2,1,0:T(4,128)S(1)} async-done(((f32[64,4,128]{2,1,0:T(4,128)}), f32[64,4,128]{2,1,0:T(4,128)S(1)}, u32[]{:S(2)}, u32[]{:S(2)}) %all-to-all-start.2) | async-done | bytes 131104 | tf_op jit(solution)/shard_map/all_to_all | solution.py:16
  296.8 2.5 fusion.4
  (62 shorter events, 19.2 us)
Async XLA Ops:
  7.2 17.1 %copy-start = (bf16[8192,128]{1,0:T(8,128)(2,1)S(1)}, bf16[8192,128]{1,0:T(8,128)(2,1)}, u32[]{:S(2)}) copy-start(bf16[8192,128]{1,0:T(8,128)(2,1)} %param.7) | copy-start | bytes 6291460
  10.9 23.7 %all-to-all-start = ((f32[64,4,256]{2,1,0:T(4,128)}), f32[64,4,256]{2,1,0:T(4,128)S(1)}, u32[]{:S(2)}, u32[]{:S(2)}) async-start(f32[64,4,256]{2,1,0:T(4,128)} %broadcast_in_dim.21), calls=%async_computation | async-start | bytes 524288 | tf_op jit(solution)/shard_map/all_to_all | solution.py:16
  30.8 24.2 %copy-start.3 = (s32[4,1]{0,1:T(1,128)S(1)}, s32[4,1]{0,1:T(1,128)}, u32[]{:S(2)}) copy-start(s32[4,1]{0,1:T(1,128)} %param.9) | copy-start | bytes 52
  34.7 179.1 %all-to-all-start.1 = ((bf16[64,256,128]{2,1,0:T(8,128)(2,1)}), bf16[64,256,128]{2,1,0:T(8,128)(2,1)}, u32[]{:S(2)}, u32[]{:S(2)}) async-start(bf16[64,256,128]{2,1,0:T(8,128)(2,1)} %copy.30), calls=%async_computation.1 | async-start | bytes 8388608 | tf_op jit(solution)/shard_map/all_to_all | solution.py:58
  41.4 255.4 %all-gather.2.cloned.1.call-start = ((), (), s32[]{:S(2)}) async-start(), calls=%async_computation.3 | async-start | bytes 1179648 | tf_op jit(solution)/shard_map/all_gather | solution.py:59
  41.5 4.6 %collective-permute-start = (f32[256,256]{1,0:T(8,128)S(1)}, f32[256,256]{1,0:T(8,128)S(1)}, u32[]{:S(2)}, u32[]{:S(2)}) collective-permute-start(f32[256,256]{1,0:T(8,128)S(1)} %reshape.65), channel_id=1, source_target_pairs={{0,1},{1,0},{2,3},{3,2},{4,5},{5,4},{6,7},{7,6},{8,9},{9,8},{10,11... | collective-permute-start | bytes 786440 | tf_op jit(solution)/shard_map/ppermute | solution.py:23
  46.1 83.4 %collective-permute-start.1 = (f32[256,256]{1,0:T(8,128)S(1)}, f32[256,256]{1,0:T(8,128)S(1)}, u32[]{:S(2)}, u32[]{:S(2)}) collective-permute-start(f32[256,256]{1,0:T(8,128)S(1)} %add.60), channel_id=1, source_target_pairs={{0,2},{1,3},{2,0},{3,1},{4,6},{5,7},{6,4},{7,5},{8,10},{9,11},{10,... | collective-permute-start | bytes 786440 | tf_op jit(solution)/shard_map/ppermute | solution.py:23
  129.6 17.3 %collective-permute-start.2 = (f32[256,256]{1,0:T(8,128)S(1)}, f32[256,256]{1,0:T(8,128)S(1)}, u32[]{:S(2)}, u32[]{:S(2)}) collective-permute-start(f32[256,256]{1,0:T(8,128)S(1)} %add.61), channel_id=1, source_target_pairs={{0,4},{1,5},{2,6},{3,7},{4,0},{5,1},{6,2},{7,3},{8,12},{9,13},{10,... | collective-permute-start | bytes 786440 | tf_op jit(solution)/shard_map/ppermute | solution.py:23
  147.5 0.7 copy-start.2
  213.8 74.3 %copy-start.1 = (f32[128,256]{1,0:T(8,128)S(1)}, f32[128,256]{1,0:T(8,128)}, u32[]{:S(2)}) copy-start(f32[128,256]{1,0:T(8,128)} %param.10) | copy-start | bytes 393220
  221.5 74.6 %all-to-all-start.2 = ((f32[64,4,128]{2,1,0:T(4,128)}), f32[64,4,128]{2,1,0:T(4,128)S(1)}, u32[]{:S(2)}, u32[]{:S(2)}) async-start(f32[64,4,128]{2,1,0:T(4,128)} %broadcast_in_dim.24), calls=%async_computation.2 | async-start | bytes 262144 | tf_op jit(solution)/shard_map/all_to_all | solution.py:16
Sparse Core Ops, SparseCore 0:
  55.1 41.9 all-gather.1

commit v2 on v0

v2 whole, which is shorter than its diff:
```python
import functools

import jax
import jax.numpy as jnp
from jax import lax
from jax.experimental import pallas as pl
from jax.experimental.pallas import tpu as pltpu
from jax.sharding import PartitionSpec as P

BLK = 256
PLANE = 16
LAYERS = 4
PICK = 4


def exact_dot(left, right):
    return jnp.dot(left, right, precision=lax.Precision.HIGHEST, preferred_element_type=jnp.float32)


def pack_kernel(count, tgt_ref, contrib_ref, out_ref, sems):
    here = lax.axis_index("row")

    def copy(b):
        dest = tgt_ref[here * count + b] // LAYERS
        away = (dest // PLANE) ^ (here // PLANE)
        return pltpu.make_async_copy(contrib_ref.at[b], out_ref.at[dest % PLANE, away], sems.at[b])

    for b in range(count):
        copy(b).start()
    for b in range(count):
        copy(b).wait()


def pack(target, pieces):
    count, rows, cols = pieces.shape
    return pl.pallas_call(
        functools.partial(pack_kernel, count),
        out_shape=jax.ShapeDtypeStruct((PLANE, LAYERS, rows, cols), pieces.dtype),
        grid_spec=pltpu.PrefetchScalarGridSpec(
            num_scalar_prefetch=1,
            grid=(),
            in_specs=[pl.BlockSpec(memory_space=pltpu.VMEM)],
            out_specs=pl.BlockSpec(memory_space=pl.ANY),
            scratch_shapes=[pltpu.SemaphoreType.DMA((count,))],
        ),
        compiler_params=pltpu.CompilerParams(vmem_limit_bytes=48 << 20),
        cost_estimate=pl.CostEstimate(flops=0, bytes_accessed=4 << 20, transcendentals=0),
        name="pack",
    )(target, pieces)


def fold_kernel(kind_ref, off_ref, spot_ref, arrived_ref, front_ref, mine_ref, other_ref, *outs):
    sums, row_ref, upper_ref = outs[:LAYERS], outs[LAYERS], outs[LAYERS + 1]
    lanes = arrived_ref.shape[3]
    layer = lax.axis_index("row") // PLANE
    for away, out in enumerate(sums):
        out[...] = jnp.zeros_like(out)
        for s in range(PLANE):
            kind = kind_ref[s * LAYERS + away]

            @pl.when(kind >= 0)
            def _():
                spot = pl.ds(pl.multiple_of(jnp.maximum(kind, 0) * BLK, BLK), BLK)
                out[spot, :] = out[spot, :] + arrived_ref[s, away].astype(jnp.float32)

        for i in range(PICK):
            picked = out[pl.ds(off_ref[away * PICK + i], 1), :]
            if away == 0:
                picked = picked + front_ref[i : i + 1, :]
            upper_ref[pl.ds((layer ^ away) * PICK + i, 1), :] = picked
    row_ref[:, :lanes] = upper_ref[...]
    half, width = mine_ref.shape
    line = lax.broadcasted_iota(jnp.int32, (row_ref.shape[0], width), 0)
    inside = lax.broadcasted_iota(jnp.int32, (8, width), 0)
    pivot_rows = jnp.zeros((row_ref.shape[0], width), jnp.float32)
    for i in range(PICK):
        spot = spot_ref[i]
        tile = pl.ds(pl.multiple_of(spot % half // 8 * 8, 8), 8)
        rows = jnp.where(spot < half, mine_ref[tile, :], other_ref[tile, :])
        row = jnp.sum(jnp.where(inside == spot % 8, rows, 0.0), axis=0, keepdims=True)
        pivot_rows = pivot_rows + jnp.where(line == layer * PICK + i, row, 0.0)
    row_ref[:, lanes:] = pivot_rows


def fold(kinds, offsets, spots, arrived, front_picked, mine, other):
    _, _, rows, cols = arrived.shape
    whole = jax.ShapeDtypeStruct((LAYERS * rows, cols), jnp.float32)
    vmem = pl.BlockSpec(memory_space=pltpu.VMEM)
    return pl.pallas_call(
        fold_kernel,
        out_shape=(whole,) * LAYERS
        + (jax.ShapeDtypeStruct((LAYERS * PICK, cols + mine.shape[1]), jnp.float32),),
        grid_spec=pltpu.PrefetchScalarGridSpec(
            num_scalar_prefetch=3, grid=(), in_specs=[vmem] * 4, out_specs=(vmem,) * (LAYERS + 1),
            scratch_shapes=[pltpu.VMEM((LAYERS * PICK, cols), jnp.float32)],
        ),
        compiler_params=pltpu.CompilerParams(vmem_limit_bytes=24 << 20),
        cost_estimate=pl.CostEstimate(flops=4 << 20, bytes_accessed=7 << 20, transcendentals=0),
        name="fold",
    )(kinds, offsets, spots, arrived, front_picked, mine, other)


def finish_kernel(mask_ref, got_ref, place_ref, mine_ref, other_ref, front_ref, near_ref, lower_ref, kept_ref, a_ref, x_ref):
    n, lanes = a_ref.shape[0], front_ref.shape[1]
    given = got_ref[:, :, lanes:].reshape(n, n)
    turned = given.T
    a = given * (1.0 / jnp.max(jnp.abs(given), axis=1, keepdims=True))
    scale = 1.0 / jnp.max(jnp.abs(turned), axis=0, keepdims=True)
    size = jnp.max(jnp.sum(jnp.abs(a), axis=1)) * jnp.max(jnp.sum(jnp.abs(a), axis=0))
    a_ref[...] = a
    x_ref[...] = turned * scale * (1.0 / size)
    rows = lax.broadcasted_iota(jnp.int32, (n, n), 0)
    eye = (rows == lax.broadcasted_iota(jnp.int32, (n, n), 1)).astype(jnp.float32)

    def going(state):
        step, now, before = state
        stalled = (now < 0.01) & (now > 0.25 * before)
        return (step < 90) & (now > 4e-8) & jnp.logical_not(stalled)

    def improve(state):
        step, now, _ = state
        x = x_ref[...]
        residual = eye - exact_dot(a_ref[...], x)
        x_ref[...] = x + exact_dot(x, residual)
        return step + 1, jnp.sum(residual * residual), now

    lax.while_loop(going, improve, (jnp.int32(0), jnp.float32(1e6), jnp.float32(1e12)))
    inverse = x_ref[...] * scale
    solved = exact_dot(inverse, got_ref[:, :, :lanes].reshape(n, lanes))
    here = lax.axis_index("col")
    part = lower_ref.shape[0]
    around = mine_ref.shape[0] // part
    for across, panel_ref in enumerate((mine_ref, other_ref)):
        for turn in range(around):
            update = exact_dot(panel_ref[turn * part : (turn + 1) * part, :], solved)
            owner = (here // 2 + turn) % around * 2 + (here % 2 + across) % 2
            spot = pl.ds(pl.multiple_of(owner * part, part), part)
            keep = mask_ref[owner * part // BLK].astype(jnp.float32)
            kept_ref[spot, :] = front_ref[spot, :] + near_ref[spot, :] - keep * update
    order = (rows == place_ref[...]).astype(jnp.float32)
    lower_ref[...] = exact_dot(mine_ref[:part, :], exact_dot(inverse, order))


def finish(mask, got, place, mine, other, front, near, part):
    n = place.shape[0]
    vmem = pl.BlockSpec(memory_space=pltpu.VMEM)
    return pl.pallas_call(
        finish_kernel,
        out_shape=(jax.ShapeDtypeStruct((part, n), jnp.float32), jax.ShapeDtypeStruct(front.shape, jnp.float32)),
        grid_spec=pltpu.PrefetchScalarGridSpec(
            num_scalar_prefetch=1,
            grid=(),
            in_specs=[vmem] * 6,
            out_specs=(vmem, vmem),
            scratch_shapes=[pltpu.VMEM((n, n), jnp.float32), pltpu.VMEM((n, n), jnp.float32)],
        ),
        compiler_params=pltpu.CompilerParams(vmem_limit_bytes=24 << 20),
        cost_estimate=pl.CostEstimate(flops=0, bytes_accessed=0, transcendentals=0),
        name="finish",
    )(mask, got, place.reshape(1, n), mine, other, front, near)


def share_panel(panel):
    count = lax.axis_size("col")
    around = count // 2
    half = panel.shape[0] // 2

    def turn(value, by):
        return lax.ppermute(value, "col", [(c, (c // 2 + by) % around * 2 + c % 2) for c in range(count)])

    before, after = turn(panel, 1), turn(panel, -1)
    far_low, far_high = turn(before[:half], 1), turn(after[half:], -1)
    mine = jnp.concatenate([panel, after, far_low, far_high, before])
    return mine, lax.ppermute(mine, "col", [(c, c ^ 1) for c in range(count)])


def body(front, contrib, target, mask, panel, pivots):
    row_count = lax.axis_size("row")
    col_count = lax.axis_size("col")
    row_index = lax.axis_index("row")
    col_index = lax.axis_index("col")
    layer = row_index // PLANE
    tile_rows, tile_cols = front.shape
    blocks_own = tile_rows // BLK
    sent_count = contrib.shape[0] // BLK
    width = pivots.shape[0]
    planes = [[z * PLANE + i for i in range(PLANE)] for z in range(LAYERS)]

    def over_plane(value):
        return lax.all_to_all(
            value, "row", split_axis=0, concat_axis=0, axis_index_groups=planes, tiled=True
        )

    def along_z(value, away):
        return lax.ppermute(value, "row", [(r, r ^ (away * PLANE)) for r in range(row_count)])

    rank = jnp.sum((pivots[:, None] > pivots[None, :]).astype(jnp.int32), axis=1)
    groups = row_index ^ (jnp.arange(LAYERS, dtype=jnp.int32) * PLANE)
    slots = (groups[:, None] * PICK + jnp.arange(PICK, dtype=jnp.int32)[None, :]).reshape(-1)
    chosen = jnp.sum(jnp.where(rank[None, :] == slots[:, None], pivots[None, :], 0), axis=1)
    offsets = chosen - jnp.repeat(groups, PICK) * tile_rows

    plane_targets = lax.dynamic_slice_in_dim(target.reshape(row_count, sent_count), layer * PLANE, PLANE, 0)
    hit = (plane_targets // blocks_own)[:, None, :] == groups[None, :, None]
    kinds = jnp.sum(jnp.where(hit, (plane_targets % blocks_own + 1)[:, None, :], 0), axis=2).reshape(-1) - 1

    arrived = over_plane(pack(target, contrib.reshape(sent_count, BLK, tile_cols)))
    panel_rows = panel.shape[0]
    mine, other = share_panel(panel)
    owner, around = offsets[:PICK] // panel_rows, col_count // 2
    turns = (owner // 2 - col_index // 2) % around
    across = (owner + col_index) % 2
    spots = (across * around + turns) * panel_rows + offsets[:PICK] % panel_rows
    picker = (offsets[:PICK, None] == jnp.arange(tile_rows, dtype=jnp.int32)[None, :]).astype(jnp.float32)
    front_picked = exact_dot(picker, front)
    place = (rank // PICK) % PLANE * (LAYERS * PICK) + rank // (PICK * PLANE) * PICK + rank % PICK
    arrived, place = lax.optimization_barrier((arrived, place))

    near0, near1, far2, far3, lines = fold(kinds, offsets, spots, arrived, front_picked, mine, other)
    lines = lines + along_z(lines, 1) + along_z(lines, 2) + along_z(lines, 3)
    lines, near1, far2, far3 = lax.optimization_barrier((lines, near1, far2, far3))
    got1, got2, got3 = along_z(near1, 1), along_z(far2, 2), along_z(far3, 3)
    got = over_plane(jnp.broadcast_to(lines[None], (PLANE,) + lines.shape))
    lower_own, kept = finish(mask.reshape(-1), got, place, mine, other, front, near0, panel_rows)
    return (lower_own, kept + got1 + (got2 + got3))


def solution(mesh):
    placed = (P("row", "col"), P("row", "col"), P(), P("row", "col"), P(("row", "col"), None), P())
    return jax.shard_map(
        body,
        mesh=mesh,
        in_specs=placed,
        out_specs=(P(("row", "col"), None), P("row", "col")),
        check_vma=False,
    )
```

time: 1230 us -> 142 us (0.12)
  the two profiles are of different devices: /device:TPU:2 before, /device:TPU:160 now
where the time goes in v2:
time: 142 us; the launch traced here: 141 us
  waiting for transfers between devices  55.7 us (39%)
  starting transfers between devices  50.2 us (35%)
  Pallas kernels  15.7 us (11%)
  blocking collectives  13.7 us (10%)
  local copies, waits for them, and re-layouts  2.87 us (2%)
  other arithmetic  1.65 us (1%)
    all_to_all x1, waiting for transfers between devices, over_plane(): lax.all_to_all(value, 'row', split_axis=0, concat_axis=0, axis_index_grou...  21.2 us
    ppermute x6, starting transfers between devices, along_z(): lax.ppermute(value, 'row', [(r, r ^ away * PLANE) for r in range(row_coun...  20.6 us
    ppermute x4, starting transfers between devices, turn(): lax.ppermute(value, 'col', [(c, (c // 2 + by) % around * 2 + c % 2) for c...  20.5 us
    ppermute x4, waiting for transfers between devices, turn(): lax.ppermute(value, 'col', [(c, (c // 2 + by) % around * 2 + c % 2) for c...  17.8 us
    ppermute x6, waiting for transfers between devices, along_z(): lax.ppermute(value, 'row', [(r, r ^ away * PLANE) for r in range(row_coun...  16.6 us
    all_to_all x1, blocking collectives, over_plane(): lax.all_to_all(value, 'row', split_axis=0, concat_axis=0, axis_index_grou...  13.7 us
    pallas_call x1, Pallas kernels, finish(): pl.pallas_call(finish_kernel, out_shape=(jax.ShapeDtypeStruct((part, n),...  9.43 us
    all_to_all x1, starting transfers between devices, over_plane(): lax.all_to_all(value, 'row', split_axis=0, concat_axis=0, axis_index_grou...  7.18 us
  transfers between devices with their start and end apart: 12, of which 7 were waited for; matrix products, arithmetic and copies ran while one was open for 1% of the time, Pallas kernels for 7%

profile of v2, /device:TPU:160, one launch (start us, length us, event | category | flops | bytes accessed | tf_op | source)
XLA Modules:
  0.0 141.1 jit_solution(4094948766106285855)
XLA Ops:
  0.6 1.6 %copy-done.1 = bf16[8192,128]{1,0:T(8,128)(2,1)S(1)} copy-done((bf16[8192,128]{1,0:T(8,128)(2,1)S(1)}, bf16[8192,128]{1,0:T(8,128)(2,1)}, u32[]{:S(2)}) %copy-start.1) | copy-done | bytes 2097176
  2.9 2.4 %pack.1 = bf16[16,4,256,128]{3,2,1,0:T(8,128)(2,1)} custom-call(s32[2048]{0:T(1024)S(1)} %copy-done.2, bf16[32,256,128]{2,1,0:T(8,128)(2,1)S(1)} %bitcast.4), custom_call_target="tpu_custom_call" | custom-call | bytes 4194304 | tf_op jit(solution)/shard_map/pack/pallas_call | solution.py:36
  5.4 7.2 %all-to-all-start = ((bf16[16,4,256,128]{3,2,1,0:T(8,128)(2,1)}), bf16[16,4,256,128]{3,2,1,0:T(8,128)(2,1)}, u32[]{:S(2)}, u32[]{:S(2)}) async-start(bf16[16,4,256,128]{3,2,1,0:T(8,128)(2,1)} %pack.1), calls=%async_computation | async-start | bytes 8388608 | tf_op jit(solution)/shard_map/all_to_all | solution.py:190
  12.6 1.9 %collective-permute-start = (f32[128,256]{1,0:T(8,128)S(1)}, f32[128,256]{1,0:T(8,128)S(1)}, u32[]{:S(2)}, u32[]{:S(2)}) collective-permute-start(f32[128,256]{1,0:T(8,128)S(1)} %copy-done.5), channel_id=1, source_target_pairs={{0,6},{1,7},{2,0},{3,1},{4,2},{5,3},{6,4},{7,5},{8,14},{9,15},{10,... | collective-permute-start | bytes 393224 | tf_op jit(solution)/shard_map/ppermute | solution.py:169
  14.5 8.2 %collective-permute-start.1 = (f32[128,256]{1,0:T(8,128)S(1)}, f32[128,256]{1,0:T(8,128)S(1)}, u32[]{:S(2)}, u32[]{:S(2)}) collective-permute-start(f32[128,256]{1,0:T(8,128)S(1)} %copy-done.5), channel_id=1, source_target_pairs={{0,2},{1,3},{2,4},{3,5},{4,6},{5,7},{6,0},{7,1},{8,10},{9,11},{10,... | collective-permute-start | bytes 393224 | tf_op jit(solution)/shard_map/ppermute | solution.py:169
  23.8 8.4 %collective-permute-done.1 = f32[128,256]{1,0:T(8,128)S(1)} collective-permute-done((f32[128,256]{1,0:T(8,128)S(1)}, f32[128,256]{1,0:T(8,128)S(1)}, u32[]{:S(2)}, u32[]{:S(2)}) %collective-permute-start.1) | collective-permute-done | bytes 131104 | tf_op jit(solution)/shard_map/ppermute | solution.py:169
  32.2 6.6 %collective-permute-start.2 = (f32[64,256]{1,0:T(8,128)S(1)}, f32[64,256]{1,0:T(8,128)S(1)}, u32[]{:S(2)}, u32[]{:S(2)}) collective-permute-start(f32[64,256]{1,0:T(8,128)S(1)} %slice.14), channel_id=1, source_target_pairs={{0,2},{1,3},{2,4},{3,5},{4,6},{5,7},{6,0},{7,1},{8,10},{9,11},{10,... | collective-permute-start | bytes 196616 | tf_op jit(solution)/shard_map/ppermute | solution.py:169
  38.8 3.8 %collective-permute-start.3 = (f32[64,256]{1,0:T(8,128)S(1)}, f32[64,256]{1,0:T(8,128)S(1)}, u32[]{:S(2)}, u32[]{:S(2)}) collective-permute-start(f32[64,256]{1,0:T(8,128)S(1)} %slice.15), channel_id=1, source_target_pairs={{0,6},{1,7},{2,0},{3,1},{4,2},{5,3},{6,4},{7,5},{8,14},{9,15},{10,... | collective-permute-start | bytes 196616 | tf_op jit(solution)/shard_map/ppermute | solution.py:169
  43.0 9.1 %collective-permute-done.3 = f32[64,256]{1,0:T(8,128)S(1)} collective-permute-done((f32[64,256]{1,0:T(8,128)S(1)}, f32[64,256]{1,0:T(8,128)S(1)}, u32[]{:S(2)}, u32[]{:S(2)}) %collective-permute-start.3) | collective-permute-done | bytes 65568 | tf_op jit(solution)/shard_map/ppermute | solution.py:169
  52.1 1.9 %collective-permute-start.4 = (f32[512,256]{1,0:T(8,128)S(1)}, f32[512,256]{1,0:T(8,128)S(1)}, u32[]{:S(2)}, u32[]{:S(2)}) collective-permute-start(f32[512,256]{1,0:T(8,128)S(1)} %constant_dynamic-update-slice_fusion.mine_ref), channel_id=1, source_target_pairs={{0,1},{1,0},{2,3},{3,2},{4,5},{5,4},{6,7},{7,6},{8,9},{9,8},{10,11... | collective-permute-start | bytes 1572872 | tf_op jit(solution)/shard_map/ppermute | solution.py:174
  54.6 21.2 %all-to-all-done.arrived_ref = bf16[16,4,256,128]{3,2,1,0:T(8,128)(2,1)} async-done(((bf16[16,4,256,128]{3,2,1,0:T(8,128)(2,1)}), bf16[16,4,256,128]{3,2,1,0:T(8,128)(2,1)}, u32[]{:S(2)}, u32[]{:S(2)}) %all-to-all-start) | async-done | bytes 4194336 | tf_op jit(solution)/shard_map/all_to_all | solution.py:190
  75.8 3.9 %fold.1 = (f32[1024,128]{1,0:T(8,128)S(1)}, f32[1024,128]{1,0:T(8,128)S(1)}, f32[1024,128]{1,0:T(8,128)S(1)}, f32[1024,128]{1,0:T(8,128)S(1)}, f32[16,384]{1,0:T(8,128)S(1)}) custom-call(s32[64]{0:T(128)S(1)} %sub.48.kind_ref, s32[16]{0:T(128)S(1)} %sub.49.off_ref, s32[4]{0:T(128)S(1)} %get-tuple-element.31.spot_ref, ...), custom_call_target="tpu_custom_call" | custom-call | flops 4194304 | bytes 7340032 | tf_op jit(solution)/shard_map/fold/pallas_call | solution.py:89
  79.7 3.9 %collective-permute-start.7 = (f32[16,384]{1,0:T(8,128)S(1)}, f32[16,384]{1,0:T(8,128)S(1)}, u32[]{:S(2)}, u32[]{:S(2)}) collective-permute-start(f32[16,384]{1,0:T(8,128)S(1)} %get-tuple-element.16), channel_id=1, source_target_pairs={{0,384},{8,392},{16,400},{24,408},{32,416},{40,424},{48,432},{56,4... | collective-permute-start | bytes 73736 | tf_op jit(solution)/shard_map/ppermute | solution.py:195
  83.6 3.2 %collective-permute-start.6 = (f32[16,384]{1,0:T(8,128)S(1)}, f32[16,384]{1,0:T(8,128)S(1)}, u32[]{:S(2)}, u32[]{:S(2)}) collective-permute-start(f32[16,384]{1,0:T(8,128)S(1)} %get-tuple-element.16), channel_id=1, source_target_pairs={{0,256},{8,264},{16,272},{24,280},{32,288},{40,296},{48,304},{56,3... | collective-permute-start | bytes 73736 | tf_op jit(solution)/shard_map/ppermute | solution.py:195
  86.8 3.4 %collective-permute-start.5 = (f32[16,384]{1,0:T(8,128)S(1)}, f32[16,384]{1,0:T(8,128)S(1)}, u32[]{:S(2)}, u32[]{:S(2)}) collective-permute-start(f32[16,384]{1,0:T(8,128)S(1)} %get-tuple-element.16), channel_id=1, source_target_pairs={{0,128},{8,136},{16,144},{24,152},{32,160},{40,168},{48,176},{56,1... | collective-permute-start | bytes 73736 | tf_op jit(solution)/shard_map/ppermute | solution.py:195
  90.2 2.3 %collective-permute-done.5 = f32[16,384]{1,0:T(8,128)S(1)} collective-permute-done((f32[16,384]{1,0:T(8,128)S(1)}, f32[16,384]{1,0:T(8,128)S(1)}, u32[]{:S(2)}, u32[]{:S(2)}) %collective-permute-start.5) | collective-permute-done | bytes 24608 | tf_op jit(solution)/shard_map/ppermute | solution.py:195
  92.5 4.3 %collective-permute-start.9 = (f32[1024,128]{1,0:T(8,128)S(1)}, f32[1024,128]{1,0:T(8,128)S(1)}, u32[]{:S(2)}, u32[]{:S(2)}) collective-permute-start(f32[1024,128]{1,0:T(8,128)S(1)} %get-tuple-element.26), channel_id=1, source_target_pairs={{0,256},{8,264},{16,272},{24,280},{32,288},{40,296},{48,304},{56,3... | collective-permute-start | bytes 1572872 | tf_op jit(solution)/shard_map/ppermute | solution.py:195
  96.8 2.5 %collective-permute-start.10 = (f32[1024,128]{1,0:T(8,128)S(1)}, f32[1024,128]{1,0:T(8,128)S(1)}, u32[]{:S(2)}, u32[]{:S(2)}) collective-permute-start(f32[1024,128]{1,0:T(8,128)S(1)} %get-tuple-element.27), channel_id=1, source_target_pairs={{0,384},{8,392},{16,400},{24,408},{32,416},{40,424},{48,432},{56,4... | collective-permute-start | bytes 1572872 | tf_op jit(solution)/shard_map/ppermute | solution.py:195
  99.3 3.4 %collective-permute-start.8 = (f32[1024,128]{1,0:T(8,128)S(1)}, f32[1024,128]{1,0:T(8,128)S(1)}, u32[]{:S(2)}, u32[]{:S(2)}) collective-permute-start(f32[1024,128]{1,0:T(8,128)S(1)} %get-tuple-element.25), channel_id=1, source_target_pairs={{0,128},{8,136},{16,144},{24,152},{32,160},{40,168},{48,176},{56,1... | collective-permute-start | bytes 1572872 | tf_op jit(solution)/shard_map/ppermute | solution.py:195
  102.7 13.7 %all_to_all.10.got_ref = f32[16,16,384]{2,1,0:T(8,128)S(1)} all-to-all(f32[16,16,384]{2,1,0:T(8,128)S(1)} %broadcast_in_dim.49), channel_id=1, replica_groups={{0,8,16,24,32,40,48,56,64,72,80,88,96,104,112,120},{128,136,144,152,160..., dimensions={0} | all-to-all | bytes 786432 | tf_op jit(solution)/shard_map/all_to_all | solution.py:190
  116.4 9.4 %finish.1 = (f32[128,256]{1,0:T(8,128)}, f32[1024,128]{1,0:T(8,128)S(1)}) custom-call(s32[4]{0:T(128)S(1)} %bitcast.6, f32[16,16,384]{2,1,0:T(8,128)S(1)} %all_to_all.10.got_ref, s32[1,256]{1,0:T(1,128)S(1)} %bitcast.5, f32[512,256]{1,0:T(8,128)S(1)} %constant_dynamic-update-slice_fusion.mine_ref, f32[512,256]{1,0:T(8,128)S(1)} %collective-permute-done.4.other_ref, ...), custom_call_target="tpu_custom_call" | custom-call | tf_op jit(solution)/shard_map/finish/pallas_call | solution.py:147
  125.9 3.4 %collective-permute-done.9 = f32[1024,128]{1,0:T(8,128)S(1)} collective-permute-done((f32[1024,128]{1,0:T(8,128)S(1)}, f32[1024,128]{1,0:T(8,128)S(1)}, u32[]{:S(2)}, u32[]{:S(2)}) %collective-permute-start.9) | collective-permute-done | bytes 524320 | tf_op jit(solution)/shard_map/ppermute | solution.py:195
  129.2 10.9 %collective-permute-done.10 = f32[1024,128]{1,0:T(8,128)S(1)} collective-permute-done((f32[1024,128]{1,0:T(8,128)S(1)}, f32[1024,128]{1,0:T(8,128)S(1)}, u32[]{:S(2)}, u32[]{:S(2)}) %collective-permute-start.10) | collective-permute-done | bytes 524320 | tf_op jit(solution)/shard_map/ppermute | solution.py:195
  140.2 0.9 add_add_fusion
  (47 shorter events, 2.7 us)
Async XLA Ops:
  0.6 1.6 %copy-start.1 = (bf16[8192,128]{1,0:T(8,128)(2,1)S(1)}, bf16[8192,128]{1,0:T(8,128)(2,1)}, u32[]{:S(2)}) copy-start(bf16[8192,128]{1,0:T(8,128)(2,1)} %param.7) | copy-start | bytes 6291460
  2.2 0.7 copy-start.2
  5.3 7.2 %copy-start.5 = (f32[128,256]{1,0:T(8,128)S(1)}, f32[128,256]{1,0:T(8,128)}, u32[]{:S(2)}) copy-start(f32[128,256]{1,0:T(8,128)} %param.10) | copy-start | bytes 393220
  5.3 17.4 %copy-start.3 = (s32[2048]{0:T(1024)S(1)}, s32[2048]{0:T(1024)}, u32[]{:S(2)}) copy-start(s32[2048]{0:T(1024)} %tgt_ref.1) | copy-start | bytes 24580
  5.4 17.9 %copy-start.6 = (s32[256]{0:T(256)S(1)}, s32[256]{0:T(256)}, u32[]{:S(2)}) copy-start(s32[256]{0:T(256)} %param.11) | copy-start | bytes 3076
  5.4 48.9 %copy-start = (f32[1024,128]{1,0:T(8,128)S(1)}, f32[1024,128]{1,0:T(8,128)}, u32[]{:S(2)}) copy-start(f32[1024,128]{1,0:T(8,128)} %front_ref.1) | copy-start | bytes 1572868
  5.4 70.4 %all-to-all-start = ((bf16[16,4,256,128]{3,2,1,0:T(8,128)(2,1)}), bf16[16,4,256,128]{3,2,1,0:T(8,128)(2,1)}, u32[]{:S(2)}, u32[]{:S(2)}) async-start(bf16[16,4,256,128]{3,2,1,0:T(8,128)(2,1)} %pack.1), calls=%async_computation | async-start | bytes 8388608 | tf_op jit(solution)/shard_map/all_to_all | solution.py:190
  12.6 26.1 %collective-permute-start = (f32[128,256]{1,0:T(8,128)S(1)}, f32[128,256]{1,0:T(8,128)S(1)}, u32[]{:S(2)}, u32[]{:S(2)}) collective-permute-start(f32[128,256]{1,0:T(8,128)S(1)} %copy-done.5), channel_id=1, source_target_pairs={{0,6},{1,7},{2,0},{3,1},{4,2},{5,3},{6,4},{7,5},{8,14},{9,15},{10,... | collective-permute-start | bytes 393224 | tf_op jit(solution)/shard_map/ppermute | solution.py:169
  14.5 17.6 %collective-permute-start.1 = (f32[128,256]{1,0:T(8,128)S(1)}, f32[128,256]{1,0:T(8,128)S(1)}, u32[]{:S(2)}, u32[]{:S(2)}) collective-permute-start(f32[128,256]{1,0:T(8,128)S(1)} %copy-done.5), channel_id=1, source_target_pairs={{0,2},{1,3},{2,4},{3,5},{4,6},{5,7},{6,0},{7,1},{8,10},{9,11},{10,... | collective-permute-start | bytes 393224 | tf_op jit(solution)/shard_map/ppermute | solution.py:169
  23.8 92.6 %copy-start.4 = (s32[4,1]{0,1:T(1,128)S(1)}, s32[4,1]{0,1:T(1,128)}, u32[]{:S(2)}) copy-start(s32[4,1]{0,1:T(1,128)} %param.9) | copy-start | bytes 52
  32.2 10.8 %collective-permute-start.2 = (f32[64,256]{1,0:T(8,128)S(1)}, f32[64,256]{1,0:T(8,128)S(1)}, u32[]{:S(2)}, u32[]{:S(2)}) collective-permute-start(f32[64,256]{1,0:T(8,128)S(1)} %slice.14), channel_id=1, source_target_pairs={{0,2},{1,3},{2,4},{3,5},{4,6},{5,7},{6,0},{7,1},{8,10},{9,11},{10,... | collective-permute-start | bytes 196616 | tf_op jit(solution)/shard_map/ppermute | solution.py:169
  38.8 13.3 %collective-permute-start.3 = (f32[64,256]{1,0:T(8,128)S(1)}, f32[64,256]{1,0:T(8,128)S(1)}, u32[]{:S(2)}, u32[]{:S(2)}) collective-permute-start(f32[64,256]{1,0:T(8,128)S(1)} %slice.15), channel_id=1, source_target_pairs={{0,6},{1,7},{2,0},{3,1},{4,2},{5,3},{6,4},{7,5},{8,14},{9,15},{10,... | collective-permute-start | bytes 196616 | tf_op jit(solution)/shard_map/ppermute | solution.py:169
  52.1 23.7 %collective-permute-start.4 = (f32[512,256]{1,0:T(8,128)S(1)}, f32[512,256]{1,0:T(8,128)S(1)}, u32[]{:S(2)}, u32[]{:S(2)}) collective-permute-start(f32[512,256]{1,0:T(8,128)S(1)} %constant_dynamic-update-slice_fusion.mine_ref), channel_id=1, source_target_pairs={{0,1},{1,0},{2,3},{3,2},{4,5},{5,4},{6,7},{7,6},{8,9},{9,8},{10,11... | collective-permute-start | bytes 1572872 | tf_op jit(solution)/shard_map/ppermute | solution.py:174
  79.7 10.5 %collective-permute-start.7 = (f32[16,384]{1,0:T(8,128)S(1)}, f32[16,384]{1,0:T(8,128)S(1)}, u32[]{:S(2)}, u32[]{:S(2)}) collective-permute-start(f32[16,384]{1,0:T(8,128)S(1)} %get-tuple-element.16), channel_id=1, source_target_pairs={{0,384},{8,392},{16,400},{24,408},{32,416},{40,424},{48,432},{56,4... | collective-permute-start | bytes 73736 | tf_op jit(solution)/shard_map/ppermute | solution.py:195
  83.6 6.6 %collective-permute-start.6 = (f32[16,384]{1,0:T(8,128)S(1)}, f32[16,384]{1,0:T(8,128)S(1)}, u32[]{:S(2)}, u32[]{:S(2)}) collective-permute-start(f32[16,384]{1,0:T(8,128)S(1)} %get-tuple-element.16), channel_id=1, source_target_pairs={{0,256},{8,264},{16,272},{24,280},{32,288},{40,296},{48,304},{56,3... | collective-permute-start | bytes 73736 | tf_op jit(solution)/shard_map/ppermute | solution.py:195
  86.8 5.7 %collective-permute-start.5 = (f32[16,384]{1,0:T(8,128)S(1)}, f32[16,384]{1,0:T(8,128)S(1)}, u32[]{:S(2)}, u32[]{:S(2)}) collective-permute-start(f32[16,384]{1,0:T(8,128)S(1)} %get-tuple-element.16), channel_id=1, source_target_pairs={{0,128},{8,136},{16,144},{24,152},{32,160},{40,168},{48,176},{56,1... | collective-permute-start | bytes 73736 | tf_op jit(solution)/shard_map/ppermute | solution.py:195
  92.5 36.7 %collective-permute-start.9 = (f32[1024,128]{1,0:T(8,128)S(1)}, f32[1024,128]{1,0:T(8,128)S(1)}, u32[]{:S(2)}, u32[]{:S(2)}) collective-permute-start(f32[1024,128]{1,0:T(8,128)S(1)} %get-tuple-element.26), channel_id=1, source_target_pairs={{0,256},{8,264},{16,272},{24,280},{32,288},{40,296},{48,304},{56,3... | collective-permute-start | bytes 1572872 | tf_op jit(solution)/shard_map/ppermute | solution.py:195
  96.8 43.4 %collective-permute-start.10 = (f32[1024,128]{1,0:T(8,128)S(1)}, f32[1024,128]{1,0:T(8,128)S(1)}, u32[]{:S(2)}, u32[]{:S(2)}) collective-permute-start(f32[1024,128]{1,0:T(8,128)S(1)} %get-tuple-element.27), channel_id=1, source_target_pairs={{0,384},{8,392},{16,400},{24,408},{32,416},{40,424},{48,432},{56,4... | collective-permute-start | bytes 1572872 | tf_op jit(solution)/shard_map/ppermute | solution.py:195
  99.3 40.9 %collective-permute-start.8 = (f32[1024,128]{1,0:T(8,128)S(1)}, f32[1024,128]{1,0:T(8,128)S(1)}, u32[]{:S(2)}, u32[]{:S(2)}) collective-permute-start(f32[1024,128]{1,0:T(8,128)S(1)} %get-tuple-element.25), channel_id=1, source_target_pairs={{0,128},{8,136},{16,144},{24,152},{32,160},{40,168},{48,176},{56,1... | collective-permute-start | bytes 1572872 | tf_op jit(solution)/shard_map/ppermute | solution.py:195

commit v3 on v2

--- a/solution.py
+++ b/solution.py
@@ -17,18 +17,24 @@
     return jnp.dot(left, right, precision=lax.Precision.HIGHEST, preferred_element_type=jnp.float32)
 
 
-def pack_kernel(count, tgt_ref, contrib_ref, out_ref, sems):
+def pack_kernel(count, tgt_ref, contrib_ref, out_ref, held_ref, sems):
     here = lax.axis_index("row")
 
-    def copy(b):
-        dest = tgt_ref[here * count + b] // LAYERS
-        away = (dest // PLANE) ^ (here // PLANE)
-        return pltpu.make_async_copy(contrib_ref.at[b], out_ref.at[dest % PLANE, away], sems.at[b])
+    def bring(b):
+        return pltpu.make_async_copy(contrib_ref.at[b], held_ref.at[b], sems.at[0, b])
+
+    def send(b):
+        dest = tgt_ref[here * count + b] >> 2
+        away = (dest >> 4) ^ (here >> 4)
+        return pltpu.make_async_copy(held_ref.at[b], out_ref.at[dest & (PLANE - 1), away], sems.at[1, b])
 
     for b in range(count):
-        copy(b).start()
+        bring(b).start()
     for b in range(count):
-        copy(b).wait()
+        bring(b).wait()
+        send(b).start()
+    for b in range(count):
+        send(b).wait()
 
 
 def pack(target, pieces):
@@ -39,11 +45,14 @@
         grid_spec=pltpu.PrefetchScalarGridSpec(
             num_scalar_prefetch=1,
             grid=(),
-            in_specs=[pl.BlockSpec(memory_space=pltpu.VMEM)],
-            out_specs=pl.BlockSpec(memory_space=pl.ANY),
-            scratch_shapes=[pltpu.SemaphoreType.DMA((count,))],
+            in_specs=[pl.BlockSpec(memory_space=pltpu.HBM)],
+            out_specs=pl.BlockSpec(memory_space=pltpu.HBM),
+            scratch_shapes=[
+                pltpu.VMEM((count, rows, cols), pieces.dtype),
+                pltpu.SemaphoreType.DMA((2, count)),
+            ],
         ),
-        compiler_params=pltpu.CompilerParams(vmem_limit_bytes=48 << 20),
+        compiler_params=pltpu.CompilerParams(vmem_limit_bytes=60 << 20),
         cost_estimate=pl.CostEstimate(flops=0, bytes_accessed=4 << 20, transcendentals=0),
         name="pack",
     )(target, pieces)
@@ -186,10 +195,18 @@
     width = pivots.shape[0]
     planes = [[z * PLANE + i for i in range(PLANE)] for z in range(LAYERS)]
 
+    pillars = [[z * PLANE + i for z in range(LAYERS)] for i in range(PLANE)]
+
+    def exchange(value, groups_of):
+        return lax.all_to_all(
+            value, "row", split_axis=0, concat_axis=0, axis_index_groups=groups_of, tiled=True
+        )
+
     def over_plane(value):
-        return lax.all_to_all(
-            value, "row", split_axis=0, concat_axis=0, axis_index_groups=planes, tiled=True
-        )
+        return exchange(value, planes)
+
+    def over_z(value):
+        return exchange(value, pillars)
 
     def along_z(value, away):
         return lax.ppermute(value, "row", [(r, r ^ (away * PLANE)) for r in range(row_count)])
@@ -217,7 +234,7 @@
     arrived, place = lax.optimization_barrier((arrived, place))
 
     near0, near1, far2, far3, lines = fold(kinds, offsets, spots, arrived, front_picked, mine, other)
-    lines = lines + along_z(lines, 1) + along_z(lines, 2) + along_z(lines, 3)
+    lines = jnp.sum(over_z(jnp.broadcast_to(lines[None], (LAYERS,) + lines.shape)), axis=0)
     lines, near1, far2, far3 = lax.optimization_barrier((lines, near1, far2, far3))
     got1, got2, got3 = along_z(near1, 1), along_z(far2, 2), along_z(far3, 3)
     got = over_plane(jnp.broadcast_to(lines[None], (PLANE,) + lines.shape))

time: 142 us -> 139 us (0.979)
  blocking collectives: 13.7 us -> 24.4 us
  starting transfers between devices: 50.2 us -> 39.8 us
  waiting for transfers between devices: 55.7 us -> 52.9 us
  local copies, waits for them, and re-layouts: 2.87 us -> 1.39 us
    all_to_all x1 -> x2, blocking collectives: 13.7 us -> 24.4 us  [exchange(): lax.all_to_all(value, 'row', split_axis=0, concat_axis=0, axis_index_grou...]
    ppermute x6 -> x3, starting transfers between devices: 20.6 us -> 10.1 us  [along_z(): lax.ppermute(value, 'row', [(r, r ^ away * PLANE) for r in range(row_coun...]
    ppermute x6 -> x3, waiting for transfers between devices: 16.6 us -> 14 us  [along_z(): lax.ppermute(value, 'row', [(r, r ^ away * PLANE) for r in range(row_coun...]
    ppermute x4, waiting for transfers between devices: 17.8 us -> 15.3 us  [turn(): lax.ppermute(value, 'col', [(c, (c // 2 + by) % around * 2 + c % 2) for c...]
    all_to_all x1, waiting for transfers between devices: 21.2 us -> 23.6 us  [exchange(): lax.all_to_all(value, 'row', split_axis=0, concat_axis=0, axis_index_grou...]
    unnamed x18 -> x16, local copies, waits for them, and re-layouts: 2.34 us -> 0.85 us
  transfers between devices with their start and end apart: 12 -> 9, of which waited for: 7 -> 6; matrix products, arithmetic and copies ran while one was open for 1% -> 1% of each run, Pallas kernels for 7% -> 7%
where the time goes in v3:
time: 139 us; the launch traced here: 138 us
  waiting for transfers between devices  52.9 us (38%)
  starting transfers between devices  39.8 us (29%)
  blocking collectives  24.4 us (18%)
  Pallas kernels  17 us (12%)
  other arithmetic  1.65 us (1%)
    all_to_all x2, blocking collectives, exchange(): lax.all_to_all(value, 'row', split_axis=0, concat_axis=0, axis_index_grou...  24.4 us
    all_to_all x1, waiting for transfers between devices, exchange(): lax.all_to_all(value, 'row', split_axis=0, concat_axis=0, axis_index_grou...  23.6 us
    ppermute x4, starting transfers between devices, turn(): lax.ppermute(value, 'col', [(c, (c // 2 + by) % around * 2 + c % 2) for c...  20.6 us
    ppermute x4, waiting for transfers between devices, turn(): lax.ppermute(value, 'col', [(c, (c // 2 + by) % around * 2 + c % 2) for c...  15.3 us
    ppermute x3, waiting for transfers between devices, along_z(): lax.ppermute(value, 'row', [(r, r ^ away * PLANE) for r in range(row_coun...  14 us
    ppermute x3, starting transfers between devices, along_z(): lax.ppermute(value, 'row', [(r, r ^ away * PLANE) for r in range(row_coun...  10.1 us
    pallas_call x1, Pallas kernels, finish(): pl.pallas_call(finish_kernel, out_shape=(jax.ShapeDtypeStruct((part, n),...  9.46 us
    all_to_all x1, starting transfers between devices, exchange(): lax.all_to_all(value, 'row', split_axis=0, concat_axis=0, axis_index_grou...  7.21 us
  transfers between devices with their start and end apart: 9, of which 6 were waited for; matrix products, arithmetic and copies ran while one was open for 1% of the time, Pallas kernels for 7%

profile of v3, /device:TPU:160, one launch (start us, length us, event | category | flops | bytes accessed | tf_op | source)
XLA Modules:
  0.0 138.3 jit_solution(4475166788048407026)
XLA Ops:
  0.6 3.7 %pack.1 = bf16[16,4,256,128]{3,2,1,0:T(8,128)(2,1)} custom-call(s32[2048]{0:T(1024)} %tgt_ref.1, bf16[32,256,128]{2,1,0:T(8,128)(2,1)} %bitcast.6), custom_call_target="tpu_custom_call" | custom-call | bytes 4194304 | tf_op jit(solution)/shard_map/pack/pallas_call | solution.py:42
  4.3 7.2 %all-to-all-start = ((bf16[16,4,256,128]{3,2,1,0:T(8,128)(2,1)}), bf16[16,4,256,128]{3,2,1,0:T(8,128)(2,1)}, u32[]{:S(2)}, u32[]{:S(2)}) async-start(bf16[16,4,256,128]{3,2,1,0:T(8,128)(2,1)} %pack.1), calls=%async_computation | async-start | bytes 8388608 | tf_op jit(solution)/shard_map/all_to_all | solution.py:201
  11.6 1.9 %collective-permute-start = (f32[128,256]{1,0:T(8,128)S(1)}, f32[128,256]{1,0:T(8,128)S(1)}, u32[]{:S(2)}, u32[]{:S(2)}) collective-permute-start(f32[128,256]{1,0:T(8,128)S(1)} %copy-done.3), channel_id=1, source_target_pairs={{0,6},{1,7},{2,0},{3,1},{4,2},{5,3},{6,4},{7,5},{8,14},{9,15},{10,... | collective-permute-start | bytes 393224 | tf_op jit(solution)/shard_map/ppermute | solution.py:178
  13.5 8.2 %collective-permute-start.1 = (f32[128,256]{1,0:T(8,128)S(1)}, f32[128,256]{1,0:T(8,128)S(1)}, u32[]{:S(2)}, u32[]{:S(2)}) collective-permute-start(f32[128,256]{1,0:T(8,128)S(1)} %copy-done.3), channel_id=1, source_target_pairs={{0,2},{1,3},{2,4},{3,5},{4,6},{5,7},{6,0},{7,1},{8,10},{9,11},{10,... | collective-permute-start | bytes 393224 | tf_op jit(solution)/shard_map/ppermute | solution.py:178
  22.0 0.2 select_reduce_fusion
  22.8 8.4 %collective-permute-done.1 = f32[128,256]{1,0:T(8,128)S(1)} collective-permute-done((f32[128,256]{1,0:T(8,128)S(1)}, f32[128,256]{1,0:T(8,128)S(1)}, u32[]{:S(2)}, u32[]{:S(2)}) %collective-permute-start.1) | collective-permute-done | bytes 131104 | tf_op jit(solution)/shard_map/ppermute | solution.py:178
  31.2 6.7 %collective-permute-start.2 = (f32[64,256]{1,0:T(8,128)S(1)}, f32[64,256]{1,0:T(8,128)S(1)}, u32[]{:S(2)}, u32[]{:S(2)}) collective-permute-start(f32[64,256]{1,0:T(8,128)S(1)} %slice.14), channel_id=1, source_target_pairs={{0,2},{1,3},{2,4},{3,5},{4,6},{5,7},{6,0},{7,1},{8,10},{9,11},{10,... | collective-permute-start | bytes 196616 | tf_op jit(solution)/shard_map/ppermute | solution.py:178
  37.9 3.8 %collective-permute-start.3 = (f32[64,256]{1,0:T(8,128)S(1)}, f32[64,256]{1,0:T(8,128)S(1)}, u32[]{:S(2)}, u32[]{:S(2)}) collective-permute-start(f32[64,256]{1,0:T(8,128)S(1)} %slice.15), channel_id=1, source_target_pairs={{0,6},{1,7},{2,0},{3,1},{4,2},{5,3},{6,4},{7,5},{8,14},{9,15},{10,... | collective-permute-start | bytes 196616 | tf_op jit(solution)/shard_map/ppermute | solution.py:178
  41.7 0.5 collective-permute-done.2
  42.2 6.5 %collective-permute-done.3 = f32[64,256]{1,0:T(8,128)S(1)} collective-permute-done((f32[64,256]{1,0:T(8,128)S(1)}, f32[64,256]{1,0:T(8,128)S(1)}, u32[]{:S(2)}, u32[]{:S(2)}) %collective-permute-start.3) | collective-permute-done | bytes 65568 | tf_op jit(solution)/shard_map/ppermute | solution.py:178
  48.7 1.9 %collective-permute-start.4 = (f32[512,256]{1,0:T(8,128)S(1)}, f32[512,256]{1,0:T(8,128)S(1)}, u32[]{:S(2)}, u32[]{:S(2)}) collective-permute-start(f32[512,256]{1,0:T(8,128)S(1)} %constant_dynamic-update-slice_fusion.mine_ref), channel_id=1, source_target_pairs={{0,1},{1,0},{2,3},{3,2},{4,5},{5,4},{6,7},{7,6},{8,9},{9,8},{10,11... | collective-permute-start | bytes 1572872 | tf_op jit(solution)/shard_map/ppermute | solution.py:183
  50.9 0.3 fusion.front_ref
  51.2 23.6 %all-to-all-done.arrived_ref = bf16[16,4,256,128]{3,2,1,0:T(8,128)(2,1)} async-done(((bf16[16,4,256,128]{3,2,1,0:T(8,128)(2,1)}), bf16[16,4,256,128]{3,2,1,0:T(8,128)(2,1)}, u32[]{:S(2)}, u32[]{:S(2)}) %all-to-all-start) | async-done | bytes 4194336 | tf_op jit(solution)/shard_map/all_to_all | solution.py:201
  74.8 3.9 %fold.1 = (f32[1024,128]{1,0:T(8,128)S(1)}, f32[1024,128]{1,0:T(8,128)S(1)}, f32[1024,128]{1,0:T(8,128)S(1)}, f32[1024,128]{1,0:T(8,128)S(1)}, f32[16,384]{1,0:T(8,128)S(1)}) custom-call(s32[64]{0:T(128)S(1)} %sub.48.kind_ref, s32[16]{0:T(128)S(1)} %sub.49.off_ref, s32[4]{0:T(128)S(1)} %get-tuple-element.31.spot_ref, ...), custom_call_target="tpu_custom_call" | custom-call | flops 4194304 | bytes 7340032 | tf_op jit(solution)/shard_map/fold/pallas_call | solution.py:98
  78.7 0.8 copy-done.2
  79.5 10.7 %all_to_all.15 = f32[4,16,384]{2,1,0:T(8,128)S(1)} all-to-all(f32[4,16,384]{2,1,0:T(8,128)S(1)} %broadcast_in_dim.35), channel_id=1, replica_groups={{0,128,256,384},{8,136,264,392},{16,144,272,400},{24,152,280,408},{32,1..., dimensions={0} | all-to-all | bytes 196608 | tf_op jit(solution)/shard_map/all_to_all | solution.py:201
  90.1 2.4 %collective-permute-start.6 = (f32[1024,128]{1,0:T(8,128)}, f32[1024,128]{1,0:T(8,128)S(1)}, u32[]{:S(2)}, u32[]{:S(2)}) collective-permute-start(f32[1024,128]{1,0:T(8,128)} %copy-done.2), channel_id=1, source_target_pairs={{0,256},{8,264},{16,272},{24,280},{32,288},{40,296},{48,304},{56,3... | collective-permute-start | bytes 1572872 | tf_op jit(solution)/shard_map/ppermute | solution.py:212
  92.6 3.8 %collective-permute-start.7 = (f32[1024,128]{1,0:T(8,128)S(1)}, f32[1024,128]{1,0:T(8,128)S(1)}, u32[]{:S(2)}, u32[]{:S(2)}) collective-permute-start(f32[1024,128]{1,0:T(8,128)S(1)} %get-tuple-element.27), channel_id=1, source_target_pairs={{0,384},{8,392},{16,400},{24,408},{32,416},{40,424},{48,432},{56,4... | collective-permute-start | bytes 1572872 | tf_op jit(solution)/shard_map/ppermute | solution.py:212
  96.4 3.9 %collective-permute-start.5 = (f32[1024,128]{1,0:T(8,128)S(1)}, f32[1024,128]{1,0:T(8,128)S(1)}, u32[]{:S(2)}, u32[]{:S(2)}) collective-permute-start(f32[1024,128]{1,0:T(8,128)S(1)} %get-tuple-element.25), channel_id=1, source_target_pairs={{0,128},{8,136},{16,144},{24,152},{32,160},{40,168},{48,176},{56,1... | collective-permute-start | bytes 1572872 | tf_op jit(solution)/shard_map/ppermute | solution.py:212
  100.3 13.7 %all_to_all.16.got_ref = f32[16,16,384]{2,1,0:T(8,128)S(1)} all-to-all(f32[16,16,384]{2,1,0:T(8,128)S(1)} %broadcast_in_dim.56), channel_id=1, replica_groups={{0,8,16,24,32,40,48,56,64,72,80,88,96,104,112,120},{128,136,144,152,160..., dimensions={0} | all-to-all | bytes 786432 | tf_op jit(solution)/shard_map/all_to_all | solution.py:201
  114.0 9.5 %finish.1 = (f32[128,256]{1,0:T(8,128)}, f32[1024,128]{1,0:T(8,128)S(1)}) custom-call(s32[4]{0:T(128)S(1)} %bitcast.5, f32[16,16,384]{2,1,0:T(8,128)S(1)} %all_to_all.16.got_ref, s32[1,256]{1,0:T(1,128)S(1)} %bitcast.4, f32[512,256]{1,0:T(8,128)S(1)} %constant_dynamic-update-slice_fusion.mine_ref, f32[512,256]{1,0:T(8,128)S(1)} %collective-permute-done.4.other_ref, ...), custom_call_target="tpu_custom_call" | custom-call | tf_op jit(solution)/shard_map/finish/pallas_call | solution.py:156
  123.5 1.3 collective-permute-done.6
  124.8 12.6 %collective-permute-done.7 = f32[1024,128]{1,0:T(8,128)S(1)} collective-permute-done((f32[1024,128]{1,0:T(8,128)S(1)}, f32[1024,128]{1,0:T(8,128)S(1)}, u32[]{:S(2)}, u32[]{:S(2)}) %collective-permute-start.7) | collective-permute-done | bytes 524320 | tf_op jit(solution)/shard_map/ppermute | solution.py:212
  137.4 0.9 add_add_fusion
  (41 shorter events, 1.2 us)
Async XLA Ops:
  4.3 7.3 %copy-start.3 = (f32[128,256]{1,0:T(8,128)S(1)}, f32[128,256]{1,0:T(8,128)}, u32[]{:S(2)}) copy-start(f32[128,256]{1,0:T(8,128)} %param.10) | copy-start | bytes 393220
  4.3 17.4 %copy-start.4 = (s32[2048]{0:T(1024)S(1)}, s32[2048]{0:T(1024)}, u32[]{:S(2)}) copy-start(s32[2048]{0:T(1024)} %tgt_ref.1) | copy-start | bytes 24580
  4.3 17.9 %copy-start.5 = (s32[256]{0:T(256)S(1)}, s32[256]{0:T(256)}, u32[]{:S(2)}) copy-start(s32[256]{0:T(256)} %param.11) | copy-start | bytes 3076
  4.3 46.5 %copy-start = (f32[1024,128]{1,0:T(8,128)S(1)}, f32[1024,128]{1,0:T(8,128)}, u32[]{:S(2)}) copy-start(f32[1024,128]{1,0:T(8,128)} %front_ref.1) | copy-start | bytes 1572868
  4.3 70.4 %all-to-all-start = ((bf16[16,4,256,128]{3,2,1,0:T(8,128)(2,1)}), bf16[16,4,256,128]{3,2,1,0:T(8,128)(2,1)}, u32[]{:S(2)}, u32[]{:S(2)}) async-start(bf16[16,4,256,128]{3,2,1,0:T(8,128)(2,1)} %pack.1), calls=%async_computation | async-start | bytes 8388608 | tf_op jit(solution)/shard_map/all_to_all | solution.py:201
  11.6 26.3 %collective-permute-start = (f32[128,256]{1,0:T(8,128)S(1)}, f32[128,256]{1,0:T(8,128)S(1)}, u32[]{:S(2)}, u32[]{:S(2)}) collective-permute-start(f32[128,256]{1,0:T(8,128)S(1)} %copy-done.3), channel_id=1, source_target_pairs={{0,6},{1,7},{2,0},{3,1},{4,2},{5,3},{6,4},{7,5},{8,14},{9,15},{10,... | collective-permute-start | bytes 393224 | tf_op jit(solution)/shard_map/ppermute | solution.py:178
  13.5 17.7 %collective-permute-start.1 = (f32[128,256]{1,0:T(8,128)S(1)}, f32[128,256]{1,0:T(8,128)S(1)}, u32[]{:S(2)}, u32[]{:S(2)}) collective-permute-start(f32[128,256]{1,0:T(8,128)S(1)} %copy-done.3), channel_id=1, source_target_pairs={{0,2},{1,3},{2,4},{3,5},{4,6},{5,7},{6,0},{7,1},{8,10},{9,11},{10,... | collective-permute-start | bytes 393224 | tf_op jit(solution)/shard_map/ppermute | solution.py:178
  31.2 82.8 %copy-start.1 = (s32[4,1]{0,1:T(1,128)S(1)}, s32[4,1]{0,1:T(1,128)}, u32[]{:S(2)}) copy-start(s32[4,1]{0,1:T(1,128)} %param.9) | copy-start | bytes 52
  31.2 11.0 %collective-permute-start.2 = (f32[64,256]{1,0:T(8,128)S(1)}, f32[64,256]{1,0:T(8,128)S(1)}, u32[]{:S(2)}, u32[]{:S(2)}) collective-permute-start(f32[64,256]{1,0:T(8,128)S(1)} %slice.14), channel_id=1, source_target_pairs={{0,2},{1,3},{2,4},{3,5},{4,6},{5,7},{6,0},{7,1},{8,10},{9,11},{10,... | collective-permute-start | bytes 196616 | tf_op jit(solution)/shard_map/ppermute | solution.py:178
  37.9 10.8 %collective-permute-start.3 = (f32[64,256]{1,0:T(8,128)S(1)}, f32[64,256]{1,0:T(8,128)S(1)}, u32[]{:S(2)}, u32[]{:S(2)}) collective-permute-start(f32[64,256]{1,0:T(8,128)S(1)} %slice.15), channel_id=1, source_target_pairs={{0,6},{1,7},{2,0},{3,1},{4,2},{5,3},{6,4},{7,5},{8,14},{9,15},{10,... | collective-permute-start | bytes 196616 | tf_op jit(solution)/shard_map/ppermute | solution.py:178
  48.7 26.1 %collective-permute-start.4 = (f32[512,256]{1,0:T(8,128)S(1)}, f32[512,256]{1,0:T(8,128)S(1)}, u32[]{:S(2)}, u32[]{:S(2)}) collective-permute-start(f32[512,256]{1,0:T(8,128)S(1)} %constant_dynamic-update-slice_fusion.mine_ref), channel_id=1, source_target_pairs={{0,1},{1,0},{2,3},{3,2},{4,5},{5,4},{6,7},{7,6},{8,9},{9,8},{10,11... | collective-permute-start | bytes 1572872 | tf_op jit(solution)/shard_map/ppermute | solution.py:183
  78.7 0.8 copy-start.2
  90.1 34.7 %collective-permute-start.6 = (f32[1024,128]{1,0:T(8,128)}, f32[1024,128]{1,0:T(8,128)S(1)}, u32[]{:S(2)}, u32[]{:S(2)}) collective-permute-start(f32[1024,128]{1,0:T(8,128)} %copy-done.2), channel_id=1, source_target_pairs={{0,256},{8,264},{16,272},{24,280},{32,288},{40,296},{48,304},{56,3... | collective-permute-start | bytes 1572872 | tf_op jit(solution)/shard_map/ppermute | solution.py:212
  92.6 44.9 %collective-permute-start.7 = (f32[1024,128]{1,0:T(8,128)S(1)}, f32[1024,128]{1,0:T(8,128)S(1)}, u32[]{:S(2)}, u32[]{:S(2)}) collective-permute-start(f32[1024,128]{1,0:T(8,128)S(1)} %get-tuple-element.27), channel_id=1, source_target_pairs={{0,384},{8,392},{16,400},{24,408},{32,416},{40,424},{48,432},{56,4... | collective-permute-start | bytes 1572872 | tf_op jit(solution)/shard_map/ppermute | solution.py:212
  96.4 41.1 %collective-permute-start.5 = (f32[1024,128]{1,0:T(8,128)S(1)}, f32[1024,128]{1,0:T(8,128)S(1)}, u32[]{:S(2)}, u32[]{:S(2)}) collective-permute-start(f32[1024,128]{1,0:T(8,128)S(1)} %get-tuple-element.25), channel_id=1, source_target_pairs={{0,128},{8,136},{16,144},{24,152},{32,160},{40,168},{48,176},{56,1... | collective-permute-start | bytes 1572872 | tf_op jit(solution)/shard_map/ppermute | solution.py:212

commit v4 on v3

--- a/solution.py
+++ b/solution.py
@@ -11,6 +11,7 @@
 PLANE = 16
 LAYERS = 4
 PICK = 4
+TOP = 8388600.0
 
 
 def exact_dot(left, right):
@@ -58,8 +59,57 @@
     )(target, pieces)
 
 
+def encode(total, code, scale):
+    rows = total.shape[0]
+    step = 64
+
+    def whole(start):
+        return jnp.floor(total[start : start + step, :] * scale + 0.5).astype(jnp.int32)
+
+    for start in range(0, rows // 2, step):
+        first, second = whole(start), whole(start + rows // 2)
+        code[start : start + step, :] = (first >> 8).astype(jnp.int16)
+        code[start + rows // 2 : start + rows // 2 + step, :] = (second >> 8).astype(jnp.int16)
+        both = (first & 255) + ((second & 255) << 8) - 32768
+        code[rows + start : rows + start + step, :] = both.astype(jnp.int16)
+
+
+def decode_kernel(kept_ref, unit_ref, code1_ref, code2_ref, code3_ref, out_ref):
+    layer = lax.axis_index("row") // PLANE
+    rows = out_ref.shape[0]
+    step = 64
+    for start in range(0, rows // 2, step):
+        first, second = 0.0, 0.0
+        for k, code in enumerate((code1_ref, code2_ref, code3_ref)):
+            both = code[rows + start : rows + start + step, :].astype(jnp.int32) + 32768
+            spot = unit_ref.shape[1] - 8 + k + 1
+            unit = unit_ref[layer ^ (k + 1), spot : spot + 1, : out_ref.shape[1]]
+            upper = code[start : start + step, :].astype(jnp.int32)
+            first = first + ((upper << 8) + (both & 255)).astype(jnp.float32) * unit
+            upper = code[start + rows // 2 : start + rows // 2 + step, :].astype(jnp.int32)
+            second = second + ((upper << 8) + (both >> 8)).astype(jnp.float32) * unit
+        here = slice(start, start + step)
+        out_ref[here, :] = kept_ref[here, :] + first
+        here = slice(start + rows // 2, start + rows // 2 + step)
+        out_ref[here, :] = kept_ref[here, :] + second
+
+
+def decode(kept, spread, codes):
+    vmem = pl.BlockSpec(memory_space=pltpu.VMEM)
+    return pl.pallas_call(
+        decode_kernel,
+        out_shape=jax.ShapeDtypeStruct(kept.shape, jnp.float32),
+        in_specs=[vmem] * 5,
+        out_specs=vmem,
+        compiler_params=pltpu.CompilerParams(vmem_limit_bytes=16 << 20),
+        cost_estimate=pl.CostEstimate(flops=0, bytes_accessed=0, transcendentals=0),
+        name="decode",
+    )(kept, spread, *codes)
+
+
 def fold_kernel(kind_ref, off_ref, spot_ref, arrived_ref, front_ref, mine_ref, other_ref, *outs):
-    sums, row_ref, upper_ref = outs[:LAYERS], outs[LAYERS], outs[LAYERS + 1]
+    near_ref, codes, row_ref, upper_ref, sum_ref = outs[0], outs[1:LAYERS], outs[-3], outs[-2], outs[-1]
+    sums = (near_ref,) + tuple(sum_ref.at[k] for k in range(LAYERS - 1))
     lanes = arrived_ref.shape[3]
     layer = lax.axis_index("row") // PLANE
     for away, out in enumerate(sums):
@@ -77,18 +127,27 @@
             if away == 0:
                 picked = picked + front_ref[i : i + 1, :]
             upper_ref[pl.ds((layer ^ away) * PICK + i, 1), :] = picked
-    row_ref[:, :lanes] = upper_ref[...]
+    upper_rows = upper_ref.shape[0]
+    row_ref[:upper_rows, :lanes] = upper_ref[...]
+    row_ref[upper_rows:, :] = jnp.zeros((row_ref.shape[0] - upper_rows, row_ref.shape[1]), jnp.float32)
+    for away in range(1, LAYERS):
+        total, code = sums[away], codes[away - 1]
+        peak = jnp.maximum(jnp.max(jnp.abs(total[...])), 1e-20)
+        row_ref[upper_rows + away : upper_rows + away + 1, :] = jnp.full(
+            (1, row_ref.shape[1]), peak * (1.0 / TOP), jnp.float32
+        )
+        encode(total, code, TOP / peak)
     half, width = mine_ref.shape
-    line = lax.broadcasted_iota(jnp.int32, (row_ref.shape[0], width), 0)
+    line = lax.broadcasted_iota(jnp.int32, (upper_rows, width), 0)
     inside = lax.broadcasted_iota(jnp.int32, (8, width), 0)
-    pivot_rows = jnp.zeros((row_ref.shape[0], width), jnp.float32)
+    pivot_rows = jnp.zeros((upper_rows, width), jnp.float32)
     for i in range(PICK):
         spot = spot_ref[i]
         tile = pl.ds(pl.multiple_of(spot % half // 8 * 8, 8), 8)
         rows = jnp.where(spot < half, mine_ref[tile, :], other_ref[tile, :])
         row = jnp.sum(jnp.where(inside == spot % 8, rows, 0.0), axis=0, keepdims=True)
         pivot_rows = pivot_rows + jnp.where(line == layer * PICK + i, row, 0.0)
-    row_ref[:, lanes:] = pivot_rows
+    row_ref[:upper_rows, lanes:] = pivot_rows
 
 
 def fold(kinds, offsets, spots, arrived, front_picked, mine, other):
@@ -97,11 +156,18 @@
     vmem = pl.BlockSpec(memory_space=pltpu.VMEM)
     return pl.pallas_call(
         fold_kernel,
-        out_shape=(whole,) * LAYERS
-        + (jax.ShapeDtypeStruct((LAYERS * PICK, cols + mine.shape[1]), jnp.float32),),
+        out_shape=(whole,)
+        + (jax.ShapeDtypeStruct((LAYERS * rows * 3 // 2, cols), jnp.int16),) * (LAYERS - 1)
+        + (jax.ShapeDtypeStruct((LAYERS * PICK + 8, cols + mine.shape[1]), jnp.float32),),
         grid_spec=pltpu.PrefetchScalarGridSpec(
-            num_scalar_prefetch=3, grid=(), in_specs=[vmem] * 4, out_specs=(vmem,) * (LAYERS + 1),
-            scratch_shapes=[pltpu.VMEM((LAYERS * PICK, cols), jnp.float32)],
+            num_scalar_prefetch=3,
+            grid=(),
+            in_specs=[vmem] * 4,
+            out_specs=(vmem,) * (LAYERS + 1),
+            scratch_shapes=[
+                pltpu.VMEM((LAYERS * PICK, cols), jnp.float32),
+                pltpu.VMEM((LAYERS - 1, LAYERS * rows, cols), jnp.float32),
+            ],
         ),
         compiler_params=pltpu.CompilerParams(vmem_limit_bytes=24 << 20),
         cost_estimate=pl.CostEstimate(flops=4 << 20, bytes_accessed=7 << 20, transcendentals=0),
@@ -234,12 +300,13 @@
     arrived, place = lax.optimization_barrier((arrived, place))
 
     near0, near1, far2, far3, lines = fold(kinds, offsets, spots, arrived, front_picked, mine, other)
-    lines = jnp.sum(over_z(jnp.broadcast_to(lines[None], (LAYERS,) + lines.shape)), axis=0)
+    spread = over_z(jnp.broadcast_to(lines[None], (LAYERS,) + lines.shape))
+    lines = jnp.sum(spread[:, : LAYERS * PICK], axis=0)
     lines, near1, far2, far3 = lax.optimization_barrier((lines, near1, far2, far3))
     got1, got2, got3 = along_z(near1, 1), along_z(far2, 2), along_z(far3, 3)
     got = over_plane(jnp.broadcast_to(lines[None], (PLANE,) + lines.shape))
     lower_own, kept = finish(mask.reshape(-1), got, place, mine, other, front, near0, panel_rows)
-    return (lower_own, kept + got1 + (got2 + got3))
+    return (lower_own, decode(kept, spread, (got1, got2, got3)))
 
 
 def solution(mesh):

time: 139 us -> 131 us (0.942)
  waiting for transfers between devices: 52.9 us -> 45.2 us
  Pallas kernels: 17 us -> 18.9 us
    ppermute x3, waiting for transfers between devices: 14 us -> 6.13 us  [along_z(): lax.ppermute(value, 'row', [(r, r ^ away * PLANE) for r in range(row_coun...]
    ppermute x4, waiting for transfers between devices: 15.3 us -> 20.1 us  [turn(): lax.ppermute(value, 'col', [(c, (c // 2 + by) % around * 2 + c % 2) for c...]
    all_to_all x1, waiting for transfers between devices: 23.6 us -> 19 us  [exchange(): lax.all_to_all(value, 'row', split_axis=0, concat_axis=0, axis_index_grou...]
    pallas_call x1 -> x2, Pallas kernels: 3.85 us -> 5.78 us  [the longest x1 4.58 us: fold(): pl.pallas_call(fold_kernel, out_shape=(whole,) + (jax.ShapeDtypeStruct((L...]
  transfers between devices with their start and end apart: 9 -> 9, of which waited for: 6 -> 5; matrix products, arithmetic and copies ran while one was open for 1% -> 1% of each run, Pallas kernels for 7% -> 7%
where the time goes in v4:
time: 131 us; the launch traced here: 130 us
  waiting for transfers between devices  45.2 us (35%)
  starting transfers between devices  38.8 us (30%)
  blocking collectives  24.9 us (19%)
  Pallas kernels  18.9 us (14%)
    all_to_all x2, blocking collectives, exchange(): lax.all_to_all(value, 'row', split_axis=0, concat_axis=0, axis_index_grou...  24.9 us
    ppermute x4, starting transfers between devices, turn(): lax.ppermute(value, 'col', [(c, (c // 2 + by) % around * 2 + c % 2) for c...  20.6 us
    ppermute x4, waiting for transfers between devices, turn(): lax.ppermute(value, 'col', [(c, (c // 2 + by) % around * 2 + c % 2) for c...  20.1 us
    all_to_all x1, waiting for transfers between devices, exchange(): lax.all_to_all(value, 'row', split_axis=0, concat_axis=0, axis_index_grou...  19 us
    pallas_call x1, Pallas kernels, finish(): pl.pallas_call(finish_kernel, out_shape=(jax.ShapeDtypeStruct((part, n),...  9.44 us
    ppermute x3, starting transfers between devices, along_z(): lax.ppermute(value, 'row', [(r, r ^ away * PLANE) for r in range(row_coun...  9.21 us
    all_to_all x1, starting transfers between devices, exchange(): lax.all_to_all(value, 'row', split_axis=0, concat_axis=0, axis_index_grou...  7.16 us
    ppermute x3, waiting for transfers between devices, along_z(): lax.ppermute(value, 'row', [(r, r ^ away * PLANE) for r in range(row_coun...  6.13 us
  transfers between devices with their start and end apart: 9, of which 5 were waited for; matrix products, arithmetic and copies ran while one was open for 1% of the time, Pallas kernels for 7%

profile of v4, /device:TPU:160, one launch (start us, length us, event | category | flops | bytes accessed | tf_op | source)
XLA Modules:
  0.0 130.3 jit_solution(8778995040170876640)
XLA Ops:
  0.6 3.7 %pack.1 = bf16[16,4,256,128]{3,2,1,0:T(8,128)(2,1)} custom-call(s32[2048]{0:T(1024)} %tgt_ref.1, bf16[32,256,128]{2,1,0:T(8,128)(2,1)} %bitcast.6), custom_call_target="tpu_custom_call" | custom-call | bytes 4194304 | tf_op jit(solution)/shard_map/pack/pallas_call | solution.py:43
  4.4 7.2 %all-to-all-start = ((bf16[16,4,256,128]{3,2,1,0:T(8,128)(2,1)}), bf16[16,4,256,128]{3,2,1,0:T(8,128)(2,1)}, u32[]{:S(2)}, u32[]{:S(2)}) async-start(bf16[16,4,256,128]{3,2,1,0:T(8,128)(2,1)} %pack.1), calls=%async_computation | async-start | bytes 8388608 | tf_op jit(solution)/shard_map/all_to_all | solution.py:267
  11.5 1.9 %collective-permute-start = (f32[128,256]{1,0:T(8,128)S(1)}, f32[128,256]{1,0:T(8,128)S(1)}, u32[]{:S(2)}, u32[]{:S(2)}) collective-permute-start(f32[128,256]{1,0:T(8,128)S(1)} %copy-done.2), channel_id=1, source_target_pairs={{0,6},{1,7},{2,0},{3,1},{4,2},{5,3},{6,4},{7,5},{8,14},{9,15},{10,... | collective-permute-start | bytes 393224 | tf_op jit(solution)/shard_map/ppermute | solution.py:244
  13.5 8.2 %collective-permute-start.1 = (f32[128,256]{1,0:T(8,128)S(1)}, f32[128,256]{1,0:T(8,128)S(1)}, u32[]{:S(2)}, u32[]{:S(2)}) collective-permute-start(f32[128,256]{1,0:T(8,128)S(1)} %copy-done.2), channel_id=1, source_target_pairs={{0,2},{1,3},{2,4},{3,5},{4,6},{5,7},{6,0},{7,1},{8,10},{9,11},{10,... | collective-permute-start | bytes 393224 | tf_op jit(solution)/shard_map/ppermute | solution.py:244
  22.0 0.2 select_reduce_fusion
  22.2 0.2 convert_reduce_fusion
  22.4 0.2 select_reduce_fusion.1
  22.8 8.3 %collective-permute-done.1 = f32[128,256]{1,0:T(8,128)S(1)} collective-permute-done((f32[128,256]{1,0:T(8,128)S(1)}, f32[128,256]{1,0:T(8,128)S(1)}, u32[]{:S(2)}, u32[]{:S(2)}) %collective-permute-start.1) | collective-permute-done | bytes 131104 | tf_op jit(solution)/shard_map/ppermute | solution.py:244
  31.1 6.6 %collective-permute-start.2 = (f32[64,256]{1,0:T(8,128)S(1)}, f32[64,256]{1,0:T(8,128)S(1)}, u32[]{:S(2)}, u32[]{:S(2)}) collective-permute-start(f32[64,256]{1,0:T(8,128)S(1)} %slice.18), channel_id=1, source_target_pairs={{0,2},{1,3},{2,4},{3,5},{4,6},{5,7},{6,0},{7,1},{8,10},{9,11},{10,... | collective-permute-start | bytes 196616 | tf_op jit(solution)/shard_map/ppermute | solution.py:244
  37.7 3.8 %collective-permute-start.3 = (f32[64,256]{1,0:T(8,128)S(1)}, f32[64,256]{1,0:T(8,128)S(1)}, u32[]{:S(2)}, u32[]{:S(2)}) collective-permute-start(f32[64,256]{1,0:T(8,128)S(1)} %slice.19), channel_id=1, source_target_pairs={{0,6},{1,7},{2,0},{3,1},{4,2},{5,3},{6,4},{7,5},{8,14},{9,15},{10,... | collective-permute-start | bytes 196616 | tf_op jit(solution)/shard_map/ppermute | solution.py:244
  41.6 0.5 collective-permute-done.2
  42.1 11.3 %collective-permute-done.3 = f32[64,256]{1,0:T(8,128)S(1)} collective-permute-done((f32[64,256]{1,0:T(8,128)S(1)}, f32[64,256]{1,0:T(8,128)S(1)}, u32[]{:S(2)}, u32[]{:S(2)}) %collective-permute-start.3) | collective-permute-done | bytes 65568 | tf_op jit(solution)/shard_map/ppermute | solution.py:244
  53.3 1.9 %collective-permute-start.4 = (f32[512,256]{1,0:T(8,128)S(1)}, f32[512,256]{1,0:T(8,128)S(1)}, u32[]{:S(2)}, u32[]{:S(2)}) collective-permute-start(f32[512,256]{1,0:T(8,128)S(1)} %constant_dynamic-update-slice_fusion.mine_ref), channel_id=1, source_target_pairs={{0,1},{1,0},{2,3},{3,2},{4,5},{5,4},{6,7},{7,6},{8,9},{9,8},{10,11... | collective-permute-start | bytes 1572872 | tf_op jit(solution)/shard_map/ppermute | solution.py:249
  55.5 0.3 fusion.front_ref
  55.8 19.0 %all-to-all-done.arrived_ref = bf16[16,4,256,128]{3,2,1,0:T(8,128)(2,1)} async-done(((bf16[16,4,256,128]{3,2,1,0:T(8,128)(2,1)}), bf16[16,4,256,128]{3,2,1,0:T(8,128)(2,1)}, u32[]{:S(2)}, u32[]{:S(2)}) %all-to-all-start) | async-done | bytes 4194336 | tf_op jit(solution)/shard_map/all_to_all | solution.py:267
  74.8 4.6 %fold.1 = (f32[1024,128]{1,0:T(8,128)S(1)}, s16[1536,128]{1,0:T(8,128)(2,1)S(1)}, s16[1536,128]{1,0:T(8,128)(2,1)S(1)}, s16[1536,128]{1,0:T(8,128)(2,1)S(1)}, f32[24,384]{1,0:T(8,128)S(1)}) custom-call(s32[64]{0:T(128)S(1)} %sub.48.kind_ref, s32[16]{0:T(128)S(1)} %sub.49.off_ref, s32[4]{0:T(128)S(1)} %get-tuple-element.31.spot_ref, ...), custom_call_target="tpu_custom_call" | custom-call | flops 4194304 | bytes 7340032 | tf_op jit(solution)/shard_map/fold/pallas_call | solution.py:157
  79.4 11.2 %all_to_all.15.unit_ref = f32[4,24,384]{2,1,0:T(8,128)S(1)} all-to-all(f32[4,24,384]{2,1,0:T(8,128)S(1)} %broadcast_in_dim.35), channel_id=1, replica_groups={{0,128,256,384},{8,136,264,392},{16,144,272,400},{24,152,280,408},{32,1..., dimensions={0} | all-to-all | bytes 294912 | tf_op jit(solution)/shard_map/all_to_all | solution.py:267
  90.5 3.3 %collective-permute-start.5 = (s16[1536,128]{1,0:T(8,128)(2,1)S(1)}, s16[1536,128]{1,0:T(8,128)(2,1)S(1)}, u32[]{:S(2)}, u32[]{:S(2)}) collective-permute-start(s16[1536,128]{1,0:T(8,128)(2,1)S(1)} %get-tuple-element.25), channel_id=1, source_target_pairs={{0,128},{8,136},{16,144},{24,152},{32,160},{40,168},{48,176},{56,1... | collective-permute-start | bytes 1179656 | tf_op jit(solution)/shard_map/ppermute | solution.py:278
  93.8 2.5 %collective-permute-start.6 = (s16[1536,128]{1,0:T(8,128)(2,1)S(1)}, s16[1536,128]{1,0:T(8,128)(2,1)S(1)}, u32[]{:S(2)}, u32[]{:S(2)}) collective-permute-start(s16[1536,128]{1,0:T(8,128)(2,1)S(1)} %get-tuple-element.26), channel_id=1, source_target_pairs={{0,256},{8,264},{16,272},{24,280},{32,288},{40,296},{48,304},{56,3... | collective-permute-start | bytes 1179656 | tf_op jit(solution)/shard_map/ppermute | solution.py:278
  96.4 3.4 %collective-permute-start.7 = (s16[1536,128]{1,0:T(8,128)(2,1)S(1)}, s16[1536,128]{1,0:T(8,128)(2,1)S(1)}, u32[]{:S(2)}, u32[]{:S(2)}) collective-permute-start(s16[1536,128]{1,0:T(8,128)(2,1)S(1)} %get-tuple-element.27), channel_id=1, source_target_pairs={{0,384},{8,392},{16,400},{24,408},{32,416},{40,424},{48,432},{56,4... | collective-permute-start | bytes 1179656 | tf_op jit(solution)/shard_map/ppermute | solution.py:278
  99.8 13.7 %all_to_all.16.got_ref = f32[16,16,384]{2,1,0:T(8,128)S(1)} all-to-all(f32[16,16,384]{2,1,0:T(8,128)S(1)} %broadcast_in_dim.56), channel_id=1, replica_groups={{0,8,16,24,32,40,48,56,64,72,80,88,96,104,112,120},{128,136,144,152,160..., dimensions={0} | all-to-all | bytes 786432 | tf_op jit(solution)/shard_map/all_to_all | solution.py:267
  113.6 9.4 %finish.1 = (f32[128,256]{1,0:T(8,128)}, f32[1024,128]{1,0:T(8,128)S(1)}) custom-call(s32[4]{0:T(128)S(1)} %bitcast.5, f32[16,16,384]{2,1,0:T(8,128)S(1)} %all_to_all.16.got_ref, s32[1,256]{1,0:T(1,128)S(1)} %bitcast.4, f32[512,256]{1,0:T(8,128)S(1)} %constant_dynamic-update-slice_fusion.mine_ref, f32[512,256]{1,0:T(8,128)S(1)} %collective-permute-done.4.other_ref, ...), custom_call_target="tpu_custom_call" | custom-call | tf_op jit(solution)/shard_map/finish/pallas_call | solution.py:222
  123.0 6.1 %collective-permute-done.7.code3_ref = s16[1536,128]{1,0:T(8,128)(2,1)S(1)} collective-permute-done((s16[1536,128]{1,0:T(8,128)(2,1)S(1)}, s16[1536,128]{1,0:T(8,128)(2,1)S(1)}, u32[]{:S(2)}, u32[]{:S(2)}) %collective-permute-start.7) | collective-permute-done | bytes 393248 | tf_op jit(solution)/shard_map/ppermute | solution.py:278
  129.1 1.2 decode.1
  (39 shorter events, 0.8 us)
Async XLA Ops:
  4.3 7.2 %copy-start.2 = (f32[128,256]{1,0:T(8,128)S(1)}, f32[128,256]{1,0:T(8,128)}, u32[]{:S(2)}) copy-start(f32[128,256]{1,0:T(8,128)} %param.10) | copy-start | bytes 393220
  4.3 17.3 %copy-start.3 = (s32[2048]{0:T(1024)S(1)}, s32[2048]{0:T(1024)}, u32[]{:S(2)}) copy-start(s32[2048]{0:T(1024)} %tgt_ref.1) | copy-start | bytes 24580
  4.3 17.8 %copy-start.4 = (s32[256]{0:T(256)S(1)}, s32[256]{0:T(256)}, u32[]{:S(2)}) copy-start(s32[256]{0:T(256)} %param.11) | copy-start | bytes 3076
  4.4 51.1 %copy-start = (f32[1024,128]{1,0:T(8,128)S(1)}, f32[1024,128]{1,0:T(8,128)}, u32[]{:S(2)}) copy-start(f32[1024,128]{1,0:T(8,128)} %front_ref.1) | copy-start | bytes 1572868
  4.4 70.4 %all-to-all-start = ((bf16[16,4,256,128]{3,2,1,0:T(8,128)(2,1)}), bf16[16,4,256,128]{3,2,1,0:T(8,128)(2,1)}, u32[]{:S(2)}, u32[]{:S(2)}) async-start(bf16[16,4,256,128]{3,2,1,0:T(8,128)(2,1)} %pack.1), calls=%async_computation | async-start | bytes 8388608 | tf_op jit(solution)/shard_map/all_to_all | solution.py:267
  11.5 26.2 %collective-permute-start = (f32[128,256]{1,0:T(8,128)S(1)}, f32[128,256]{1,0:T(8,128)S(1)}, u32[]{:S(2)}, u32[]{:S(2)}) collective-permute-start(f32[128,256]{1,0:T(8,128)S(1)} %copy-done.2), channel_id=1, source_target_pairs={{0,6},{1,7},{2,0},{3,1},{4,2},{5,3},{6,4},{7,5},{8,14},{9,15},{10,... | collective-permute-start | bytes 393224 | tf_op jit(solution)/shard_map/ppermute | solution.py:244
  13.5 17.6 %collective-permute-start.1 = (f32[128,256]{1,0:T(8,128)S(1)}, f32[128,256]{1,0:T(8,128)S(1)}, u32[]{:S(2)}, u32[]{:S(2)}) collective-permute-start(f32[128,256]{1,0:T(8,128)S(1)} %copy-done.2), channel_id=1, source_target_pairs={{0,2},{1,3},{2,4},{3,5},{4,6},{5,7},{6,0},{7,1},{8,10},{9,11},{10,... | collective-permute-start | bytes 393224 | tf_op jit(solution)/shard_map/ppermute | solution.py:244
  31.1 11.0 %collective-permute-start.2 = (f32[64,256]{1,0:T(8,128)S(1)}, f32[64,256]{1,0:T(8,128)S(1)}, u32[]{:S(2)}, u32[]{:S(2)}) collective-permute-start(f32[64,256]{1,0:T(8,128)S(1)} %slice.18), channel_id=1, source_target_pairs={{0,2},{1,3},{2,4},{3,5},{4,6},{5,7},{6,0},{7,1},{8,10},{9,11},{10,... | collective-permute-start | bytes 196616 | tf_op jit(solution)/shard_map/ppermute | solution.py:244
  37.7 75.8 %copy-start.1 = (s32[4,1]{0,1:T(1,128)S(1)}, s32[4,1]{0,1:T(1,128)}, u32[]{:S(2)}) copy-start(s32[4,1]{0,1:T(1,128)} %param.9) | copy-start | bytes 52
  37.7 15.6 %collective-permute-start.3 = (f32[64,256]{1,0:T(8,128)S(1)}, f32[64,256]{1,0:T(8,128)S(1)}, u32[]{:S(2)}, u32[]{:S(2)}) collective-permute-start(f32[64,256]{1,0:T(8,128)S(1)} %slice.19), channel_id=1, source_target_pairs={{0,6},{1,7},{2,0},{3,1},{4,2},{5,3},{6,4},{7,5},{8,14},{9,15},{10,... | collective-permute-start | bytes 196616 | tf_op jit(solution)/shard_map/ppermute | solution.py:244
  53.3 21.4 %collective-permute-start.4 = (f32[512,256]{1,0:T(8,128)S(1)}, f32[512,256]{1,0:T(8,128)S(1)}, u32[]{:S(2)}, u32[]{:S(2)}) collective-permute-start(f32[512,256]{1,0:T(8,128)S(1)} %constant_dynamic-update-slice_fusion.mine_ref), channel_id=1, source_target_pairs={{0,1},{1,0},{2,3},{3,2},{4,5},{5,4},{6,7},{7,6},{8,9},{9,8},{10,11... | collective-permute-start | bytes 1572872 | tf_op jit(solution)/shard_map/ppermute | solution.py:249
  90.5 32.5 %collective-permute-start.5 = (s16[1536,128]{1,0:T(8,128)(2,1)S(1)}, s16[1536,128]{1,0:T(8,128)(2,1)S(1)}, u32[]{:S(2)}, u32[]{:S(2)}) collective-permute-start(s16[1536,128]{1,0:T(8,128)(2,1)S(1)} %get-tuple-element.25), channel_id=1, source_target_pairs={{0,128},{8,136},{16,144},{24,152},{32,160},{40,168},{48,176},{56,1... | collective-permute-start | bytes 1179656 | tf_op jit(solution)/shard_map/ppermute | solution.py:278
  93.8 29.2 %collective-permute-start.6 = (s16[1536,128]{1,0:T(8,128)(2,1)S(1)}, s16[1536,128]{1,0:T(8,128)(2,1)S(1)}, u32[]{:S(2)}, u32[]{:S(2)}) collective-permute-start(s16[1536,128]{1,0:T(8,128)(2,1)S(1)} %get-tuple-element.26), channel_id=1, source_target_pairs={{0,256},{8,264},{16,272},{24,280},{32,288},{40,296},{48,304},{56,3... | collective-permute-start | bytes 1179656 | tf_op jit(solution)/shard_map/ppermute | solution.py:278
  96.4 32.8 %collective-permute-start.7 = (s16[1536,128]{1,0:T(8,128)(2,1)S(1)}, s16[1536,128]{1,0:T(8,128)(2,1)S(1)}, u32[]{:S(2)}, u32[]{:S(2)}) collective-permute-start(s16[1536,128]{1,0:T(8,128)(2,1)S(1)} %get-tuple-element.27), channel_id=1, source_target_pairs={{0,384},{8,392},{16,400},{24,408},{32,416},{40,424},{48,432},{56,4... | collective-permute-start | bytes 1179656 | tf_op jit(solution)/shard_map/ppermute | solution.py:278
